TPU v7x, 32 devices: a whole 2x2x4 slice. The times are simulated.
32 devices in a mesh: pipe: 2 (over core), expert: 16 (over z, y, x).
Axes of the slice: x: 2, y: 2, z: 4, core: 2. Of those that a mesh axis runs over, the one named last changes fastest.
Arguments:
- hidden_a: bfloat16 [2, 1024, 3584], P('pipe', 'expert'), may hold values from -6 to 6
- routes_a: int32 [2, 1024, 8], P('pipe', 'expert'), may hold values from 0 to 15, all different within a row; in each aligned block of 64 rows (0 to 63, 64 to 127, ..., all dimensions but the last counted through in order) at most 48 rows name the same one
- hidden_b: bfloat16 [2, 1024, 3584], P('pipe', 'expert'), may hold values from -6 to 6
- routes_b: int32 [2, 1024, 8], P('pipe', 'expert'), may hold values from 0 to 15, all different within a row; in each aligned block of 64 rows (0 to 63, 64 to 127, ..., all dimensions but the last counted through in order) at most 48 rows name the same one
- grad_out_b: bfloat16 [2, 1024, 3584], P('pipe', 'expert'), may hold values from -0.796875 to 0.796875
- router: bfloat16 [2, 16, 3584], P('pipe'), as said below
- w_up: bfloat16 [2, 16, 3584, 1024], P('pipe', 'expert'), as said below
- w_down: bfloat16 [2, 16, 1024, 3584], P('pipe', 'expert'), as said below
Outputs:
- layer_out_a: bfloat16 [2, 1024, 3584], P('pipe', 'expert')
- grad_in_b: bfloat16 [2, 1024, 3584], P('pipe', 'expert')
- router_grad: float32 [2, 16, 3584], P('pipe', 'expert')
Inputs may be any that keep to these rules, and one draw needn't show every extreme that they name: `routes_a`: each token names 8 different experts. Among the 64 tokens of one device no expert is named by more than 48 tokens, and in every draw some expert is named by exactly 48 tokens of some device. `routes_b`: as for routes_a. router[1 - p] equals router[p] for every p. w_up[1 - p] equals w_up[p] for every p. w_down[1 - p] equals w_down[p] for every p.
All inputs are finite; a program needn't handle non-finite values.
Results may differ from a plain program's by a relative error of at most 0.014.
Values may be sent and summed in bfloat16 or wider, within the bound.
A program may use at most 128 MiB of HBM per device.

v0:
```python
import functools

import jax
import jax.numpy as jnp
from jax import lax
from jax.experimental import pallas as pl
from jax.experimental.pallas import tpu as pltpu
from jax.sharding import PartitionSpec as P

ROUTED_SCALE = 2.5
EPSILON = 1e-06


def partner(block, axis, bit):
    count = lax.axis_size(axis)
    route = []
    for low in range(count):
        high = low | 1 << bit
        if high != low and high < count:
            route += [(low, high), (high, low)]
    return lax.ppermute(block, axis, route)


MESH = pl.DeviceIdType.MESH
DMA = pltpu.SemaphoreType.DMA
PLANE = 4


def remote(src, dst, send_sem, recv_sem, target):
    return pltpu.make_async_remote_copy(
        src_ref=src,
        dst_ref=dst,
        send_sem=send_sem,
        recv_sem=recv_sem,
        device_id={"expert": target},
        device_id_type=MESH,
    )


def place():
    me = lax.axis_index("expert")
    z, y, x = me // PLANE, (me // 2) % 2, me % 2
    return (me, z, y, x, me + 1 - 2 * x, me + 2 - 4 * y)


def greet(planes):
    me, z, y, x, x_near, y_near = place()
    barrier = pltpu.get_barrier_semaphore()
    pl.semaphore_signal(barrier, inc=1, device_id={"expert": x_near}, device_id_type=MESH)
    pl.semaphore_signal(barrier, inc=1, device_id={"expert": y_near}, device_id_type=MESH)

    @pl.when(z < planes - 1)
    def _():
        pl.semaphore_signal(barrier, inc=1, device_id={"expert": me + PLANE}, device_id_type=MESH)

    @pl.when(z > 0)
    def _():
        pl.semaphore_signal(barrier, inc=1, device_id={"expert": me - PLANE}, device_id_type=MESH)

    ends = jnp.where(z == 0, 1, 0) + jnp.where(z == planes - 1, 1, 0)
    pl.semaphore_wait(barrier, 4 - ends)


def gather_kernel(count, planes, *refs):
    ins, outs = refs[:count], refs[count : 2 * count]
    own_sem, up_s, down_s, z_r, x_s, x_r, y_s, y_r, d_s, d_r = refs[2 * count :]
    me, z, y, x, x_near, y_near = place()

    def up(k, p, src):
        return remote(src, outs[k].at[p * PLANE + y * 2 + x], up_s.at[k, p], z_r.at[k, p], me + PLANE)

    def down(k, p, src):
        return remote(src, outs[k].at[p * PLANE + y * 2 + x], down_s.at[k, p], z_r.at[k, p], me - PLANE)

    def to_x(k, p, src):
        return remote(src, outs[k].at[p * PLANE + y * 2 + x], x_s.at[k, p], x_r.at[k, p], x_near)

    def to_y(k, p, src):
        return remote(src, outs[k].at[p * PLANE + y * 2 + x], y_s.at[k, p], y_r.at[k, p], y_near)

    def half(k, p, way):
        if way == 0:
            ref = outs[k].at[p * PLANE + y * 2 + 1 - x, 0]
            return remote(ref, ref, d_s.at[k, p, 0], d_r.at[k, p, 0], y_near)
        ref = outs[k].at[p * PLANE + (1 - y) * 2 + x, 1]
        return remote(ref, ref, d_s.at[k, p, 1], d_r.at[k, p, 1], x_near)

    def each(d, act):
        if d == 0:
            act(z, 0)
            return

        @pl.when(z >= d)
        def _():
            act(z - d, 1)

        @pl.when(z + d < planes)
        def _():
            act(z + d, -1)

    def spread(k, p, way, wait):
        src = ins[k] if way == 0 else outs[k].at[p * PLANE + y * 2 + x]

        def do(copy):
            copy.wait_send() if wait else copy.start()

        if way != 0 and not wait:
            up(k, p, src).wait_recv()
        if way >= 0:

            @pl.when(z < planes - 1)
            def _():
                do(up(k, p, src))

        if way <= 0:

            @pl.when(z > 0)
            def _():
                do(down(k, p, src))

        do(to_x(k, p, src))
        do(to_y(k, p, src))

    def relay(k, p, way):
        to_x(k, p, ins[k]).wait_recv()
        half(k, p, 0).start()
        to_y(k, p, ins[k]).wait_recv()
        half(k, p, 1).start()

    def finish(k, p, way):
        for route in range(2):
            half(k, p, route).wait()
        spread(k, p, way, True)

    greet(planes)
    for k in range(count):
        pltpu.make_async_copy(ins[k], outs[k].at[me], own_sem.at[k]).start()
        each(0, lambda p, way: spread(k, p, way, False))
    for k in range(count):
        for d in range(1, planes):
            each(d, lambda p, way: spread(k, p, way, False))
            each(d - 1, lambda p, way: relay(k, p, way))
        each(planes - 1, lambda p, way: relay(k, p, way))
    for k in range(count):
        for d in range(planes):
            each(d, lambda p, way: finish(k, p, way))
        pltpu.make_async_copy(ins[k], outs[k].at[me], own_sem.at[k]).wait()


def gather_all(blocks, collective_id):
    n = lax.axis_size("expert")
    planes = n // PLANE
    count = len(blocks)
    halved = [b.reshape(2, b.shape[0] // 2, b.shape[1]) for b in blocks]
    outs = pl.pallas_call(
        functools.partial(gather_kernel, count, planes),
        out_shape=[jax.ShapeDtypeStruct((n,) + b.shape, b.dtype) for b in halved],
        in_specs=[pl.BlockSpec(memory_space=pltpu.VMEM)] * count,
        out_specs=[pl.BlockSpec(memory_space=pl.ANY)] * count,
        scratch_shapes=[DMA((count,))] + [DMA((count, planes))] * 7 + [DMA((count, planes, 2))] * 2,
        compiler_params=pltpu.CompilerParams(collective_id=collective_id, has_side_effects=True),
    )(*halved)
    return [o.reshape(n * b.shape[0], b.shape[1]) for o, b in zip(outs, blocks)]


def scatter_stages(planes, part, out, a_r, c_r, b_x, b_y, total, z_r, *sems):
    ax_s, ax_r, ay_s, ay_r, cx_s, cx_r, cy_s, cy_r, z_s, up_r, down_r = sems
    me, z, y, x, x_near, y_near = place()
    rows, cols = part.shape[2:]
    step = 16

    def slot(p, yy, xx):
        return p * PLANE + yy * 2 + xx

    def add(dst, *srcs):
        def body(i, carry):
            r = pl.ds(pl.multiple_of(i * step, step), step)
            acc = srcs[0][r, :].astype(jnp.float32)
            for s in srcs[1:]:
                acc = acc + s[r, :].astype(jnp.float32)
            dst[r, :] = acc.astype(dst.dtype)
            return carry

        lax.fori_loop(0, rows // step, body, 0)

    def diagonal(p):
        src = slot(p, 1 - y, 1 - x)
        return (
            remote(part.at[src, 0], a_r.at[p, 0], ay_s.at[p], ay_r.at[p], y_near),
            remote(part.at[src, 1], a_r.at[p, 1], ax_s.at[p], ax_r.at[p], x_near),
        )

    def beside(p):
        return (
            remote(b_x.at[p, 0], c_r.at[p, 0, 0], cx_s.at[p, 0], cx_r.at[p, 0], x_near),
            remote(part.at[slot(p, y, 1 - x), 1], c_r.at[p, 0, 1], cx_s.at[p, 1], cx_r.at[p, 1], x_near),
            remote(b_y.at[p, 0], c_r.at[p, 1, 1], cy_s.at[p, 0], cy_r.at[p, 0], y_near),
            remote(part.at[slot(p, 1 - y, x), 0], c_r.at[p, 1, 0], cy_s.at[p, 1], cy_r.at[p, 1], y_near),
        )

    def rise(p):
        return remote(total.at[p], z_r.at[0, p], z_s.at[p], up_r.at[p], me + PLANE)

    def sink(p):
        return remote(total.at[p], z_r.at[1, p], z_s.at[p], down_r.at[p], me - PLANE)

    def first(p, way):
        for copy in diagonal(p):
            copy.start()
        beside(p)[1].start()
        beside(p)[3].start()

    def second(p, way):
        to_y, to_x = diagonal(p)
        to_y.wait_recv()
        add(b_x.at[p, 0], part.at[slot(p, y, 1 - x), 0], a_r.at[p, 0])
        beside(p)[0].start()
        to_x.wait_recv()
        add(b_y.at[p, 0], part.at[slot(p, 1 - y, x), 1], a_r.at[p, 1])
        beside(p)[2].start()

    def third(p, way):
        for copy in beside(p):
            copy.wait_recv()
        for h in range(2):
            add(total.at[p, h], part.at[slot(p, y, x), h], c_r.at[p, 0, h], c_r.at[p, 1, h])

        def take(copy, level):
            copy.wait_recv()
            for h in range(2):
                add(total.at[p, h], total.at[p, h], z_r.at[level, p, h])

        if way >= 0:

            @pl.when(z > 0)
            def _():
                take(rise(p), 0)

        if way <= 0:

            @pl.when(z < planes - 1)
            def _():
                take(sink(p), 1)

        if way > 0:
            rise(p).start()
        if way < 0:
            sink(p).start()
        if way == 0:
            out[...] = total[p]

    def finish(p, way):
        for copy in diagonal(p) + beside(p):
            copy.wait_send()
        if way != 0:
            rise(p).wait_send()

    return (first, second, third, finish)


def scatter_kernel(planes, count, *refs):
    parts, outs, rest = refs[:count], refs[count : 2 * count], refs[2 * count :]
    per = len(rest) // count
    z = place()[1]
    stages = [
        scatter_stages(planes, parts[k], outs[k], *rest[k * per : (k + 1) * per])
        for k in range(count)
    ]

    def each(d, act):
        if d == 0:
            act(z, 0)
            return

        @pl.when(z >= d)
        def _():
            act(z - d, -1)

        @pl.when(z + d < planes)
        def _():
            act(z + d, 1)

    greet(planes)
    order = list(range(planes - 1, -1, -1))
    for k in range(count):
        for d in order:
            each(d, stages[k][0])
    for i, d in enumerate(order):
        for k in range(count):
            each(d, stages[k][1])
        if i > 0:
            for k in range(count):
                each(order[i - 1], stages[k][2])
    for k in range(count):
        each(0, stages[k][2])
    for k in range(count):
        for d in order:
            each(d, stages[k][3])


def scatter_sums(parts, collective_id):
    n = lax.axis_size("expert")
    planes = n // PLANE
    tokens, cols = parts[0].shape
    rows = tokens // n // 2
    half = (rows, cols)
    kind = parts[0].dtype
    count = len(parts)
    if count > 1 and count * 3 * parts[0].size * kind.itemsize > 56 << 20:
        return [scatter_sums([part], collective_id + k)[0] for k, part in enumerate(parts)]
    outs = pl.pallas_call(
        functools.partial(scatter_kernel, planes, count),
        out_shape=[jax.ShapeDtypeStruct((2,) + half, kind)] * count,
        in_specs=[pl.BlockSpec(memory_space=pltpu.VMEM)] * count,
        out_specs=[pl.BlockSpec(memory_space=pltpu.VMEM)] * count,
        scratch_shapes=(
            [
                pltpu.VMEM((planes, 2) + half, kind),
                pltpu.VMEM((planes, 2, 2) + half, kind),
                pltpu.VMEM((planes, 1) + half, kind),
                pltpu.VMEM((planes, 1) + half, kind),
                pltpu.VMEM((planes, 2) + half, kind),
                pltpu.VMEM((2, planes, 2) + half, kind),
            ]
            + [DMA((planes,))] * 4
            + [DMA((planes, 2))] * 4
            + [DMA((planes,))] * 3
        )
        * count,
        compiler_params=pltpu.CompilerParams(
            collective_id=collective_id, has_side_effects=True, vmem_limit_bytes=60 << 20
        ),
    )(*[part.reshape((n, 2) + half) for part in parts])
    return [out.reshape(2 * rows, cols) for out in outs]


def prepare(hidden, routes, router_segment):
    expert_count = router_segment.shape[0]
    hidden32 = hidden.astype(jnp.float32)
    rinv = lax.rsqrt(jnp.mean(hidden32 * hidden32, axis=-1, keepdims=True) + EPSILON)
    normed = (hidden32 * rinv).astype(jnp.bfloat16)
    logits = jnp.einsum("td,ed->te", normed, router_segment, preferred_element_type=jnp.float32)
    chosen = jnp.any(
        routes[:, :, None] == jnp.arange(expert_count, dtype=jnp.int32)[None, None, :], axis=1
    )
    affinity = jnp.where(chosen, jax.nn.sigmoid(logits), 0.0)
    return (hidden32, rinv, normed, affinity)


def on_device(hidden_a, routes_a, hidden_b, routes_b, grad_out_b, router, w_up, w_down):
    n_expert = lax.axis_size("expert")
    me = lax.axis_index("expert")
    tok_count = hidden_a.shape[1]
    router_segment = router[0]
    expert_count = router_segment.shape[0]
    local_count = w_up.shape[1]
    hidden32_a, rinv_a, normed_a, affinity_a = prepare(hidden_a[0], routes_a[0], router_segment)
    hidden32_b, rinv_b, normed_b, affinity_b = prepare(hidden_b[0], routes_b[0], router_segment)
    grad_out = grad_out_b[0]
    affinity_ab = jnp.concatenate([affinity_a, affinity_b], axis=1)
    lanes = -(-2 * expert_count // 128) * 128
    affinity_ab = jnp.pad(affinity_ab, ((0, 0), (0, lanes - 2 * expert_count)))
    rows_a, rows_b, rows_g, affinities = gather_all([normed_a, normed_b, grad_out, affinity_ab], 1)
    aff_a, aff_b = affinities[:, :expert_count], affinities[:, expert_count : 2 * expert_count]
    total_b = jnp.sum(aff_b, axis=1, keepdims=True)
    weight_a = aff_a / jnp.sum(aff_a, axis=1, keepdims=True)
    weight_b = aff_b / total_b

    def column(table, local):
        return lax.dynamic_slice_in_dim(table, me * local_count + local, 1, axis=1)

    sum_a = 0.0
    sum_b = 0.0
    scores = []
    for local in range(local_count):
        up, down = w_up[0, local], w_down[0, local]
        pre = jnp.dot(rows_a, up, preferred_element_type=jnp.float32)
        active = jax.nn.silu(pre).astype(jnp.bfloat16)
        out = jnp.dot(active, down, preferred_element_type=jnp.float32)
        sum_a = sum_a + out * column(weight_a, local)
    for local in range(local_count):
        up, down = w_up[0, local], w_down[0, local]
        pre = jnp.dot(rows_b, up, preferred_element_type=jnp.float32)
        back = jnp.einsum("td,fd->tf", rows_g, down, preferred_element_type=jnp.float32)
        sig = jax.nn.sigmoid(pre)
        scores.append(jnp.sum(back * (pre * sig), axis=-1))
        inner = (back * (sig * (1.0 + pre * (1.0 - sig)))).astype(jnp.bfloat16)
        lifted = jnp.einsum("tf,df->td", inner, up, preferred_element_type=jnp.float32)
        sum_b = sum_b + lifted * column(weight_b, local)
    sum_ab = scatter_sums([sum_a.astype(jnp.bfloat16), sum_b.astype(jnp.bfloat16)], 2)
    mixed = sum_ab[0].astype(jnp.float32)
    layer_out = (hidden32_a + ROUTED_SCALE * mixed).astype(jnp.bfloat16)

    flat = jnp.stack(scores).reshape(-1)
    padded = jnp.pad(flat, (0, -flat.shape[0] % 2048)).reshape(-1, 128)
    score = gather_all([padded], 4)[0].reshape(n_expert, -1)[:, : flat.shape[0]]
    score = score.reshape(expert_count, -1).T
    score = jnp.where(aff_b > 0.0, score, 0.0)
    gate_grad = ROUTED_SCALE * score
    logit_grad = (
        aff_b
        * (1.0 - aff_b)
        * (gate_grad - jnp.sum(gate_grad * weight_b, axis=1, keepdims=True))
        / total_b
    )
    own_columns = lax.dynamic_slice_in_dim(logit_grad, me * local_count, local_count, axis=1)
    own_term = jnp.dot(
        own_columns.T, rows_b.astype(jnp.float32), precision=lax.Precision.HIGHEST
    )
    mirrored = own_term
    for bit in range(lax.axis_size("pipe").bit_length() - 1):
        mirrored = partner(mirrored, "pipe", bit)
    router_grad = own_term + mirrored

    dense = lax.dynamic_slice_in_dim(logit_grad, me * tok_count, tok_count, axis=0)
    lifted_sum = sum_ab[1].astype(jnp.float32)
    normed_grad = ROUTED_SCALE * lifted_sum + jnp.dot(
        dense, router_segment.astype(jnp.float32), precision=lax.Precision.HIGHEST
    )
    mean_term = jnp.mean(normed_grad * hidden32_b, axis=-1, keepdims=True)
    grad_in = (
        grad_out.astype(jnp.float32) + rinv_b * normed_grad - hidden32_b * rinv_b**3 * mean_term
    )
    return (layer_out[None], grad_in.astype(jnp.bfloat16)[None], router_grad[None])


def solution(mesh):
    placed = (
        P("pipe", "expert", None),
        P("pipe", "expert", None),
        P("pipe", "expert", None),
        P("pipe", "expert", None),
        P("pipe", "expert", None),
        P("pipe", None, None),
        P("pipe", "expert", None, None),
        P("pipe", "expert", None, None),
    )
    return jax.shard_map(
        on_device,
        mesh=mesh,
        in_specs=placed,
        out_specs=(P("pipe", "expert", None), P("pipe", "expert", None), P("pipe", "expert", None)),
        check_vma=False,
    )
```

profile of v0, /device:TPU:0, one launch (start us, length us, event | category | flops | bytes accessed | tf_op | source)
XLA Modules:
  0.0 458.1 jit_solution(265663370917610062)
XLA Ops:
  0.6 0.0 copy-start
  0.6 1.2 multiply_reduce_fusion.1
  1.9 1.2 fusion.22
  3.1 0.1 rsqrt.30
  3.2 0.1 rsqrt.28
  3.3 0.7 fusion.40
  4.0 0.7 fusion.41
  4.7 0.0 copy-done
  4.7 1.3 fusion.18
  6.1 1.3 fusion.14
  7.4 0.1 copy.42
  7.5 0.6 pad.8.clone
  8.1 2.3 multiply_convert_fusion.6
  10.4 193.3 %shard_map.103 = (bf16[16,2,32,3584]{3,2,1,0:T(8,128)(2,1)}, bf16[16,2,32,3584]{3,2,1,0:T(8,128)(2,1)}, bf16[16,2,32,3584]{3,2,1,0:T(8,128)(2,1)}, f32[16,2,32,128]{3,2,1,0:T(8,128)}) custom-call(bf16[2,32,3584]{2,1,0:T(8,128)(2,1)} %get-tuple-element.28.refs_0_, bf16[2,32,3584]{2,1,0:T(8,128)(2,1)} %get-tuple-element.27.refs_1_, ...), custom_call_target="tpu_custom_call" | custom-call | tf_op jit(solution)/shard_map/pallas_call | solution.py:155
  203.7 1.7 slice_reduce_fusion
  205.4 0.2 copy.41
  205.6 11.3 %fusion.4 = f32[1024,1024]{1,0:T(8,128)S(1)} fusion(bf16[1024,3584]{1,0:T(8,128)(2,1)} %bitcast.97, bf16[1,1,3584,1024]{3,2,1,0:T(8,128)(2,1)} %param.14), kind=kOutput, calls=%fused_computation.6 | convolution fusion | flops 7516192768 | bytes 18874368 | tf_op jit(solution)/shard_map/dot_general | solution.py:383
  216.9 0.0 copy-start.4
  216.9 15.6 %multiply_reduce_fusion = (f32[1024]{0:T(1024)S(1)}, f32[1024,1024]{1,0:T(8,128)}) fusion(f32[1024,1024]{1,0:T(8,128)S(1)} %fusion.4, bf16[1024,3584]{1,0:T(8,128)(2,1)} %bitcast.116, bf16[1,1,1024,3584]{3,2,1,0:T(8,128)(2,1)} %param.15), kind=kOutput, calls=%fused_computation.11 | convolution fusion | flops 7522483200 | bytes 23072768 | tf_op jit(solution)/shard_map/td,fd->tf/dot_general | solution.py:384
  232.5 0.0 copy-done.4
  232.5 0.6 pad_bitcast_fusion.refs_0_
  233.1 17.8 %shard_map.105 = f32[16,2,8,128]{3,2,1,0:T(8,128)} custom-call(f32[2,8,128]{2,1,0:T(8,128)} %pad_bitcast_fusion.refs_0_), custom_call_target="tpu_custom_call" | custom-call | tf_op jit(solution)/shard_map/pallas_call | solution.py:155
  250.9 0.9 copy.48
  251.9 5.1 %fusion.43 = f32[1,3584]{1,0:T(1,128)S(1)} fusion(bf16[1024,3584]{1,0:T(8,128)(2,1)} %bitcast.98, f32[1024,16]{0,1:T(8,128)S(1)} %get-tuple-element.19, s32[]{:T(128)S(6)} %select_n.21), kind=kOutput, calls=%fused_computation.70 | convolution fusion | flops 44040192 | bytes 7358468 | tf_op jit(solution)/shard_map/dot_general | solution.py:407
  257.0 0.0 collective-permute-start
  257.0 12.7 %multiply_convert_fusion.3 = bf16[1024,1024]{1,0:T(8,128)(2,1)S(1)} fusion(bf16[1024,3584]{1,0:T(8,128)(2,1)} %bitcast.115, bf16[1,1,3584,1024]{3,2,1,0:T(8,128)(2,1)} %param.14), kind=kOutput, calls=%fused_computation.14 | convolution fusion | flops 7521435648 | bytes 16777216 | tf_op jit(solution)/shard_map/dot_general | solution.py:377
  269.8 0.2 constant_dynamic-slice_fusion.1
  270.0 0.2 copy.45
  270.2 16.3 %multiply_convert_fusion = bf16[1024,3584]{1,0:T(8,128)(2,1)} fusion(bf16[1,1,3584,1024]{3,2,1,0:T(8,128)(2,1)} %param.14, f32[1024]{0:T(1024)S(1)} %bitcast.114, f32[1024,1024]{1,0:T(8,128)} %get-tuple-element.24, f32[1024,1024]{1,0:T(8,128)} %copy-done.4), kind=kOutput, calls=%fused_computation | convolution fusion | flops 7532969984 | bytes 23072768 | tf_op jit(solution)/shard_map/tf,df->td/dot_general | solution.py:388
  286.6 12.8 %multiply_convert_fusion.1 = bf16[1024,3584]{1,0:T(8,128)(2,1)} fusion(bf16[1024,1024]{1,0:T(8,128)(2,1)S(1)} %multiply_convert_fusion.3, bf16[1,1,1024,3584]{3,2,1,0:T(8,128)(2,1)} %param.15, f32[1024]{0:T(1024)S(1)} %bitcast.111), kind=kOutput, calls=%fused_computation.1 | convolution fusion | flops 7523532800 | bytes 16781312 | tf_op jit(solution)/shard_map/dot_general | solution.py:379
  299.4 0.0 copy-start.1
  299.4 0.0 copy-start.3
  299.4 153.1 %shard_map.104 = (bf16[2,32,3584]{2,1,0:T(8,128)(2,1)}, bf16[2,32,3584]{2,1,0:T(8,128)(2,1)}) custom-call(bf16[16,2,32,3584]{3,2,1,0:T(8,128)(2,1)} %bitcast.100, bf16[16,2,32,3584]{3,2,1,0:T(8,128)(2,1)} %bitcast.99), custom_call_target="tpu_custom_call" | custom-call | tf_op jit(solution)/shard_map/pallas_call | solution.py:311
  452.5 0.0 copy-start.2
  452.5 1.1 convert_multiply_fusion.2
  453.6 1.1 convert_multiply_fusion.1
  454.7 0.0 copy-done.1
  454.7 0.8 fusion.24
  455.6 0.0 copy-done.3
  455.6 1.1 fusion.30
  456.6 0.0 copy-done.2
  456.6 0.8 fusion.21
  457.5 0.0 collective-permute-done
  457.5 0.6 add_bitcast_fusion
  (8 shorter events, 0.1 us)
Async XLA Ops:
  0.6 4.1 copy-start
  216.9 15.6 %copy-start.4 = (f32[1024,1024]{1,0:T(8,128)}, f32[1024,1024]{1,0:T(8,128)S(1)}, u32[]{:S(2)}) copy-start(f32[1024,1024]{1,0:T(8,128)S(1)} %fusion.4) | copy-start | bytes 12582916
  257.0 200.5 %collective-permute-start = (f32[1,3584]{1,0:T(1,128)S(1)}, f32[1,3584]{1,0:T(1,128)S(1)}, u32[]{:S(2)}, u32[]{:S(2)}) collective-permute-start(f32[1,3584]{1,0:T(1,128)S(1)} %fusion.43), channel_id=1, source_target_pairs={{0,16},{16,0},{1,17},{17,1},{2,18},{18,2},{3,19},{19,3},{4,20},{20... | collective-permute-start | bytes 43016 | tf_op jit(solution)/shard_map/ppermute | solution.py:21
  299.4 155.3 %copy-start.1 = (bf16[1,64,3584]{2,1,0:T(8,128)(2,1)S(1)}, bf16[1,64,3584]{2,1,0:T(8,128)(2,1)}, u32[]{:S(2)}) copy-start(bf16[1,64,3584]{2,1,0:T(8,128)(2,1)} %param.10) | copy-start | bytes 1376260
  299.4 156.2 %copy-start.3 = (bf16[1,64,3584]{2,1,0:T(8,128)(2,1)S(1)}, bf16[1,64,3584]{2,1,0:T(8,128)(2,1)}, u32[]{:S(2)}) copy-start(bf16[1,64,3584]{2,1,0:T(8,128)(2,1)} %param.12) | copy-start | bytes 1376260
  452.5 4.2 copy-start.2
where the time goes:
time: 459 us; the launch traced here: 458 us
  Pallas kernels  364 us (79%)
  matrix products  77.3 us (17%)
  other arithmetic  12.7 us (3%)
    pallas_call x2, Pallas kernels, gather_all(): pl.pallas_call(functools.partial(gather_kernel, count, planes), out_shape...  211 us
    pallas_call x1, Pallas kernels, scatter_sums(): pl.pallas_call(functools.partial(scatter_kernel, planes, count), out_shap...  153 us
    dot_general x1, matrix products, on_device(): jnp.einsum('tf,df->td', inner, up, preferred_element_type=jnp.float32)  16.3 us
    dot_general x1, matrix products, on_device(): jnp.einsum('td,fd->tf', rows_g, down, preferred_element_type=jnp.float32)  15.6 us
    dot_general x1, matrix products, on_device(): out = jnp.dot(active, down, preferred_element_type=jnp.float32)  12.8 us
    dot_general x1, matrix products, on_device(): pre = jnp.dot(rows_a, up, preferred_element_type=jnp.float32)  12.7 us
    dot_general x1, matrix products, on_device(): pre = jnp.dot(rows_b, up, preferred_element_type=jnp.float32)  11.3 us
  transfers between devices with their start and end apart: 1, of which 0 were waited for; matrix products, arithmetic and copies ran while one was open for 10% of the time, Pallas kernels for 33%

commit v1 on v0

--- a/solution.py
+++ b/solution.py
@@ -1,4 +1,5 @@
 import functools
+import math
 
 import jax
 import jax.numpy as jnp
@@ -424,6 +425,506 @@
     return (layer_out[None], grad_in.astype(jnp.bfloat16)[None], router_grad[None])
 
 
+def fused_kernel(dims, *refs):
+    planes, tok, depth, width, dc, n_up, n_pipe = dims
+    (a, b, g, tab, wu, wd, out, lg_out, rg_out) = refs[:9]
+    (rows, tabs, wu_b, wd_b, bu, bd, act, pre, back) = refs[9:18]
+    (o_buf, y_buf, t_buf, z_buf, sc_col, sc_own, sc_all, rg_buf, rg_in) = refs[18:27]
+    (own_s, zs, zr, ys, yr, xs, xr, ms, mr, bus, bds) = refs[27:38]
+    (rys, ryr, rzs, rzr, scs, scr, gs, gr) = refs[38:46]
+    slots = 2 * planes
+    m_rows = slots * tok
+    chunks = depth // dc
+    half_d = depth // 2
+    half_f = width // 2
+    up_rows = half_d // n_up
+    tile = 256
+    me, z, y, x, x_near, y_near = place()
+    p = lax.axis_index("pipe")
+    mirror = n_pipe - 1 - p
+    part = (2 * p) // n_pipe
+    slot_me = y * planes + z
+
+    def copy(src, dst, send, recv, expert, pipe=p):
+        return pltpu.make_async_remote_copy(
+            src_ref=src,
+            dst_ref=dst,
+            send_sem=send,
+            recv_sem=recv,
+            device_id={"pipe": pipe, "expert": expert},
+            device_id_type=MESH,
+        )
+
+    def chip(plane, row):
+        return plane * PLANE + row * 2 + x
+
+    def of_slot(s):
+        return chip(s % planes, s // planes)
+
+    barrier = pltpu.get_barrier_semaphore()
+
+    def hello(pipe, expert):
+        pl.semaphore_signal(
+            barrier, inc=1, device_id={"pipe": pipe, "expert": expert}, device_id_type=MESH
+        )
+
+    for i in range(1, slots):
+        hello(p, of_slot((slot_me + i) % slots))
+    hello(p, x_near)
+    hello(mirror, me)
+    hello(mirror, x_near)
+    pl.semaphore_wait(barrier, slots - 1 + 3)
+
+    def up_region(which, i):
+        return pl.ds(pl.multiple_of(which * half_d + i * up_rows, up_rows), up_rows)
+
+    def up_x(i):
+        r = up_region(part, i)
+        return copy(wu.at[r], wu_b.at[r], xs.at[i], xr.at[i], x_near)
+
+    def up_m(i, which):
+        r = up_region(which, i)
+        return copy(wu_b.at[r], wu_b.at[r], ms.at[i], mr.at[i], me, mirror)
+
+    def down_rows(which):
+        return pl.ds(pl.multiple_of(which * half_f, half_f), half_f)
+
+    def columns(c):
+        return pl.ds(pl.multiple_of(c * dc, dc), dc)
+
+    def down_x(c):
+        r = down_rows(part)
+        src = wd.at[r, columns(c)]
+        return copy(src, wd_b.at[c, r], xs.at[n_up + c], xr.at[n_up + c], x_near)
+
+    def down_m(c, which):
+        ref = wd_b.at[c, down_rows(which)]
+        return copy(ref, ref, ms.at[n_up + c], mr.at[n_up + c], me, mirror)
+
+    for i in range(n_up):
+        up_x(i).start()
+    for c in range(chunks):
+        down_x(c).start()
+
+    ins = [tab, a, b, g]
+    bufs = [tabs, rows.at[0], rows.at[1], rows.at[2]]
+
+    def z_copy(k, d, slot):
+        target = chip((z + d) % planes, y)
+        return copy(ins[k], bufs[k].at[slot], zs.at[k, d - 1], zr.at[k, d - 1], target)
+
+    def y_copy(k, d, row):
+        ref = bufs[k].at[row * planes + (z - d + planes) % planes]
+        src = ins[k] if isinstance(d, int) and d == 0 else ref
+        return copy(src, ref, ys.at[k, d], yr.at[k, d], y_near)
+
+    if planes == 4:
+        low, top = (3 - z) // 3, z // 3
+        sources = [1 + 2 * low, 3 - low - top, 2 - low + top]
+        targets = [1 + 2 * top, 3 - low - top, 2 + low - top]
+    else:
+        sources = targets = list(range(1, planes))
+
+    def serve(k, i):
+        d = sources[i]
+        z_copy(k, d, y * planes + (z - d + planes) % planes).wait_recv()
+        y_copy(k, d, y).start()
+
+    def arrived(k):
+        for d in range(planes):
+            y_copy(k, d, 1 - y).wait_recv()
+
+    for k in range(4):
+        y_copy(k, 0, y).start()
+        for d in targets:
+            z_copy(k, d, slot_me).start()
+    own = [pltpu.make_async_copy(ins[k], bufs[k].at[slot_me], own_s.at[k]) for k in range(4)]
+    for k in range(4):
+        own[k].start()
+
+    def chunk_of(k, c):
+        return rows[k, :, :, columns(c)].reshape(m_rows, dc)
+
+    def nn(lhs, rhs):
+        return jnp.dot(lhs, rhs, preferred_element_type=jnp.float32)
+
+    def nt(lhs, rhs):
+        return lax.dot_general(
+            lhs, rhs, (((1,), (1,)), ((), ())), preferred_element_type=jnp.float32
+        )
+
+    def load_up(c):
+        return pltpu.make_async_copy(wu.at[columns(c)], bu.at[c % 2], bus.at[c % 2])
+
+    def load_down(c):
+        return pltpu.make_async_copy(wd.at[:, columns(c)], bd.at[c % 2], bds.at[c % 2])
+
+    def next_chunk(load, c):
+        load(c).wait()
+
+        @pl.when(c + 1 < chunks)
+        def _():
+            load(c + 1).start()
+
+    def clear(dst):
+        def body(s, carry):
+            dst[pl.ds(pl.multiple_of(s * tok, tok), tok), :] = jnp.zeros((tok, width), jnp.float32)
+            return carry
+
+        lax.fori_loop(0, slots, body, 0)
+
+    def project(k, partner, dst):
+        clear(dst)
+        if not partner:
+            load_up(0).start()
+
+        def body(c, carry):
+            if not partner:
+                next_chunk(load_up, c)
+            lhs = chunk_of(k, c)
+            for n in range(width // tile):
+                cols = pl.ds(n * tile, tile)
+                rhs = wu_b[columns(c), cols] if partner else bu[c % 2, :, cols]
+                dst[:, cols] += nn(lhs, rhs)
+            return carry
+
+        lax.fori_loop(0, chunks, body, 0)
+
+    lane = lax.broadcasted_iota(jnp.int32, (tok, tabs.shape[-1]), 1)
+
+    def pick(s, column):
+        return jnp.sum(jnp.where(lane == column, tabs[s], 0.0), axis=-1, keepdims=True)
+
+    experts = 2 * slots
+    expert_of = [me, x_near]
+
+    def activate(which, src):
+        def body(s, carry):
+            r = pl.ds(pl.multiple_of(s * tok, tok), tok)
+            v = src[r, :]
+            act[which, r, :] = (v * jax.nn.sigmoid(v) * pick(s, expert_of[which])).astype(act.dtype)
+            return carry
+
+        lax.fori_loop(0, slots, body, 0)
+
+    def invert():
+        def body(s, carry):
+            r = pl.ds(pl.multiple_of(s * tok, tok), tok)
+            scores = []
+            for which in range(2):
+                v = pre[which, r, :]
+                bk = back[which, r, :]
+                sig = jax.nn.sigmoid(v)
+                scores.append(jnp.sum(bk * (v * sig), axis=-1, keepdims=True))
+                inner = bk * (sig * (1.0 + v * (1.0 - sig)))
+                weight = pick(s, experts + expert_of[which])
+                act[which, r, :] = (inner * weight).astype(act.dtype)
+            even = jnp.where(x == 0, scores[0], scores[1])
+            odd = jnp.where(x == 0, scores[1], scores[0])
+            sc_col[s] = jnp.where(lane == 0, even, jnp.where(lane == 1, odd, 0.0))
+            return carry
+
+        lax.fori_loop(0, slots, body, 0)
+        sc_own[...] = sc_col[...].reshape(m_rows, lane.shape[1]).T[:8]
+
+    steps = 2 * chunks
+
+    def rs_y(q):
+        src = o_buf.at[q, pl.ds((1 - y) * planes, planes)]
+        return copy(src, y_buf.at[q], rys.at[q], ryr.at[q], y_near)
+
+    def rs_z(q, d):
+        plane = (z + d) % planes
+        src = t_buf.at[q, plane]
+        return copy(src, z_buf.at[q, d - 1], rzs.at[q, d - 1], rzr.at[q, d - 1], chip(plane, y))
+
+    def fold_y(q):
+        rs_y(q).wait_recv()
+        for k in range(planes):
+            both = o_buf[q, y * planes + k].astype(jnp.float32) + y_buf[q, k].astype(jnp.float32)
+            t_buf[q, k] = both.astype(t_buf.dtype)
+        for d in targets:
+            rs_z(q, d).start()
+
+    def fold_z(q):
+        total = t_buf[q, z].astype(jnp.float32)
+        for d in range(1, planes):
+            rs_z(q, d).wait_recv()
+            total = total + z_buf[q, d - 1].astype(jnp.float32)
+        out[q // chunks, :, columns(q % chunks)] = total
+
+    def behind(q):
+        @pl.when(q >= 2)
+        def _():
+            fold_y(q - 2)
+
+        @pl.when(q >= 4)
+        def _():
+            fold_z(q - 4)
+
+    def store(q, n, value):
+        cols = pl.ds(n * tile, tile)
+        o_buf[q, :, :, cols] = value.reshape(slots, tok, tile).astype(o_buf.dtype)
+
+    for k in range(3):
+        for i in range(planes - 1):
+            serve(k, i)
+    for k in range(4):
+        own[k].wait()
+    arrived(0)
+    arrived(1)
+    project(0, False, back.at[0])
+    activate(0, back.at[0])
+    serve(3, 0)
+    for i in range(n_up):
+        up_x(i).wait_recv()
+        up_m(i, part).start()
+    for i in range(n_up):
+        up_m(i, 1 - part).wait_recv()
+    project(0, True, back.at[1])
+    activate(1, back.at[1])
+    for i in range(1, planes - 2):
+        serve(3, i)
+    arrived(2)
+    project(1, False, pre.at[0])
+    for i in range(max(1, planes - 2), planes - 1):
+        serve(3, i)
+    project(1, True, pre.at[1])
+    clear(back.at[0])
+    clear(back.at[1])
+    load_down(0).start()
+    down_x(0).wait_recv()
+    down_m(0, part).start()
+    arrived(3)
+
+    def forward(c, carry):
+        next_chunk(load_down, c)
+        down_m(c, 1 - part).wait_recv()
+        for n in range(dc // tile):
+            cols = pl.ds(n * tile, tile)
+            store(c, n, nn(act[0], bd[c % 2, :, cols]) + nn(act[1], wd_b[c, :, cols]))
+        rs_y(c).start()
+        lhs = chunk_of(2, c)
+        for n in range(width // tile):
+            cols = pl.ds(n * tile, tile)
+            back[0, :, cols] += nt(lhs, bd[c % 2, cols, :])
+            back[1, :, cols] += nt(lhs, wd_b[c, cols, :])
+
+        @pl.when(c + 1 < chunks)
+        def _():
+            down_x(c + 1).wait_recv()
+            down_m(c + 1, part).start()
+
+        behind(c)
+        return carry
+
+    lax.fori_loop(0, chunks, forward, 0)
+    load_up(0).start()
+    invert()
+
+    def score_copy(i, slot):
+        target = of_slot((slot_me + i) % slots)
+        return copy(sc_own, sc_all.at[slot], scs.at[i - 1], scr.at[i - 1], target)
+
+    for i in range(1, slots):
+        score_copy(i, slot_me).start()
+
+    def backward(c, carry):
+        next_chunk(load_up, c)
+        q = chunks + c
+        for n in range(dc // tile):
+            cols = pl.ds(n * tile, tile)
+            shared = pl.ds(pl.multiple_of(c * dc + n * tile, tile), tile)
+            store(q, n, nt(act[0], bu[c % 2, cols, :]) + nt(act[1], wu_b[shared, :]))
+        rs_y(q).start()
+        behind(q)
+        return carry
+
+    lax.fori_loop(0, chunks, backward, 0)
+
+    sc_all[slot_me] = sc_own[...]
+    for i in range(1, slots):
+        score_copy(i, (slot_me - i + slots) % slots).wait_recv()
+    table = tabs[...].reshape(m_rows, lane.shape[1]).T
+    lines = []
+    for e in range(experts):
+        plane, row, odd = e // PLANE, (e // 2) % 2, e % 2
+        lines.append(sc_all[row * planes + plane, odd : odd + 1, :])
+    score = jnp.concatenate(lines, axis=0)
+    gate = ROUTED_SCALE * score
+    mean = jnp.sum(gate * table[experts : 2 * experts], axis=0, keepdims=True)
+    logit = table[2 * experts : 3 * experts] * (gate - mean)
+    lg_out[...] = logit
+    order = lax.broadcasted_iota(jnp.int32, (experts, m_rows), 0)
+    mine = jnp.sum(jnp.where(order == me, logit, 0.0), axis=0, keepdims=True)
+    theirs = jnp.sum(jnp.where(order == x_near, logit, 0.0), axis=0, keepdims=True)
+    both = jnp.concatenate([mine, theirs, jnp.zeros((6, m_rows), jnp.float32)], axis=0)
+    high = both.astype(jnp.bfloat16)
+    rest = both - high.astype(jnp.float32)
+    middle = rest.astype(jnp.bfloat16)
+    last = (rest - middle.astype(jnp.float32)).astype(jnp.bfloat16)
+    for c in range(chunks):
+        cols = pl.ds(c * dc, dc)
+        rhs = rows[1, :, :, cols].reshape(m_rows, dc)
+        rg_buf[:, cols] = nn(high, rhs) + nn(middle, rhs) + nn(last, rhs)
+
+    def grad_copy(i):
+        expert = me if i == 0 else x_near
+        pipe = p if i == 1 else mirror
+        return copy(rg_buf, rg_in.at[i], gs.at[i], gr.at[i], expert, pipe)
+
+    for i in range(3):
+        grad_copy(i).start()
+    for q in range(steps - 2, steps):
+        fold_y(q)
+        fold_z(q - 2)
+    for i in range(3):
+        grad_copy(i).wait_recv()
+    rg_out[...] = rg_buf[0:1, :] + rg_in[0, 0:1, :] + rg_in[1, 1:2, :] + rg_in[2, 1:2, :]
+    for q in range(steps - 2, steps):
+        fold_z(q)
+
+    for k in range(4):
+        for d in range(1, planes):
+            z_copy(k, d, slot_me).wait_send()
+        for d in range(planes):
+            y_copy(k, d, y).wait_send()
+    for i in range(n_up):
+        up_x(i).wait_send()
+        up_m(i, part).wait_send()
+
+    def drain(c, carry):
+        down_x(c).wait_send()
+        down_m(c, part).wait_send()
+        return carry
+
+    lax.fori_loop(0, chunks, drain, 0)
+
+    def drain_rs(q, carry):
+        rs_y(q).wait_send()
+        for d in range(1, planes):
+            rs_z(q, d).wait_send()
+        return carry
+
+    lax.fori_loop(0, steps, drain_rs, 0)
+    for i in range(1, slots):
+        score_copy(i, slot_me).wait_send()
+    for i in range(3):
+        grad_copy(i).wait_send()
+
+
+N_UP = 4
+
+
+def fused_plan(n, tok, depth, width):
+    planes = n // PLANE
+    slots = 2 * planes
+    m_rows = slots * tok
+    dc = 512 if depth % 512 == 0 else 256
+    chunks = depth // dc
+    steps = 2 * chunks
+    bf, f32 = jnp.bfloat16, jnp.float32
+    buffers = [
+        ((3, slots, tok, depth), bf),
+        ((slots, tok, 128), f32),
+        ((depth, width), bf),
+        ((chunks, width, dc), bf),
+        ((2, dc, width), bf),
+        ((2, width, dc), bf),
+        ((2, m_rows, width), bf),
+        ((2, m_rows, width), f32),
+        ((2, m_rows, width), f32),
+        ((steps, slots, tok, dc), bf),
+        ((steps, planes, tok, dc), bf),
+        ((steps, planes, tok, dc), bf),
+        ((steps, planes - 1, tok, dc), bf),
+        ((slots, tok, 128), f32),
+        ((8, m_rows), f32),
+        ((slots, 8, m_rows), f32),
+        ((8, depth), f32),
+        ((3, 8, depth), f32),
+    ]
+    sems = [
+        (4,),
+        (4, planes - 1),
+        (4, planes - 1),
+        (4, planes),
+        (4, planes),
+        (N_UP + chunks,),
+        (N_UP + chunks,),
+        (N_UP + chunks,),
+        (N_UP + chunks,),
+        (2,),
+        (2,),
+        (steps,),
+        (steps,),
+        (steps, planes - 1),
+        (steps, planes - 1),
+        (slots - 1,),
+        (slots - 1,),
+        (3,),
+        (3,),
+    ]
+    total = sum(math.prod(shape) * jnp.dtype(kind).itemsize for shape, kind in buffers)
+    outs = 2 * tok * depth * 4 + 3 * tok * depth * 2
+    fits = total + outs < 64_500_000 and 3 * n <= 128
+    return fits, (planes, tok, depth, width, dc, N_UP), buffers, sems
+
+
+def fused(normed_a, normed_b, grad_out, table, up, down, plan):
+    _, dims, buffers, sems = plan
+    planes, tok, depth = dims[:3]
+    slots = 2 * planes
+    vmem = pl.BlockSpec(memory_space=pltpu.VMEM)
+    hbm = pl.BlockSpec(memory_space=pl.ANY)
+    return pl.pallas_call(
+        functools.partial(fused_kernel, dims + (lax.axis_size("pipe"),)),
+        out_shape=[
+            jax.ShapeDtypeStruct((2, tok, depth), jnp.float32),
+            jax.ShapeDtypeStruct((2 * slots, slots * tok), jnp.float32),
+            jax.ShapeDtypeStruct((1, depth), jnp.float32),
+        ],
+        in_specs=[vmem] * 4 + [hbm] * 2,
+        out_specs=[vmem] * 3,
+        scratch_shapes=[pltpu.VMEM(shape, kind) for shape, kind in buffers]
+        + [DMA(shape) for shape in sems],
+        compiler_params=pltpu.CompilerParams(
+            collective_id=7, has_side_effects=True, vmem_limit_bytes=67_000_000
+        ),
+    )(normed_a, normed_b, grad_out, table, up, down)
+
+
+def on_device_fused(
+    plan, hidden_a, routes_a, hidden_b, routes_b, grad_out_b, router, w_up, w_down
+):
+    router_segment = router[0]
+    n_expert = router_segment.shape[0]
+    planes, tok = plan[1][:2]
+    hidden32_a, rinv_a, normed_a, affinity_a = prepare(hidden_a[0], routes_a[0], router_segment)
+    hidden32_b, rinv_b, normed_b, affinity_b = prepare(hidden_b[0], routes_b[0], router_segment)
+    grad_out = grad_out_b[0]
+    total_b = jnp.sum(affinity_b, axis=1, keepdims=True)
+    weight_a = affinity_a / jnp.sum(affinity_a, axis=1, keepdims=True)
+    weight_b = affinity_b / total_b
+    slope_b = affinity_b * (1.0 - affinity_b) / total_b
+    table = jnp.concatenate([weight_a, weight_b, slope_b], axis=1)
+    table = jnp.pad(table, ((0, 0), (0, 128 - 3 * n_expert)))
+    sums, logit_grad, router_grad = fused(
+        normed_a, normed_b, grad_out, table, w_up[0, 0], w_down[0, 0], plan
+    )
+    layer_out = (hidden32_a + ROUTED_SCALE * sums[0]).astype(jnp.bfloat16)
+    _, z, y, _, _, _ = place()
+    dense = lax.dynamic_slice_in_dim(logit_grad, (y * planes + z) * tok, tok, axis=1)
+    normed_grad = ROUTED_SCALE * sums[1] + jnp.einsum(
+        "et,ed->td", dense, router_segment.astype(jnp.float32), precision=lax.Precision.HIGHEST
+    )
+    mean_term = jnp.mean(normed_grad * hidden32_b, axis=-1, keepdims=True)
+    grad_in = (
+        grad_out.astype(jnp.float32) + rinv_b * normed_grad - hidden32_b * rinv_b**3 * mean_term
+    )
+    return (layer_out[None], grad_in.astype(jnp.bfloat16)[None], router_grad[None])
+
+
 def solution(mesh):
     placed = (
         P("pipe", "expert", None),
@@ -435,8 +936,16 @@
         P("pipe", "expert", None, None),
         P("pipe", "expert", None, None),
     )
+
+    def body(*args):
+        w_up = args[6]
+        plan = fused_plan(lax.axis_size("expert"), args[0].shape[1], w_up.shape[2], w_up.shape[3])
+        if w_up.shape[1] == 1 and plan[0]:
+            return on_device_fused(plan, *args)
+        return on_device(*args)
+
     return jax.shard_map(
-        on_device,
+        body,
         mesh=mesh,
         in_specs=placed,
         out_specs=(P("pipe", "expert", None), P("pipe", "expert", None), P("pipe", "expert", None)),

time: 459 us -> 265 us (0.58)
  Pallas kernels: 364 us -> 252 us
  matrix products: 77.3 us -> 4.37 us
  other arithmetic: 12.7 us -> 6.1 us
    pallas_call x3 -> x1, Pallas kernels: 364 us -> 252 us  [fused(): pl.pallas_call(functools.partial(fused_kernel, dims + (lax.axis_size('pip...]
    dot_general x7 -> x1, matrix products: 74.7 us -> 2.45 us  [on_device_fused(): jnp.einsum('et,ed->td', dense, router_segment.astype(jnp.float32), precis...]
  transfers between devices with their start and end apart: 1 -> 0, of which waited for: 0 -> 0; matrix products, arithmetic and copies ran while one was open for 10% -> 0% of each run, Pallas kernels for 33% -> 0%
where the time goes in v1:
time: 265 us; the launch traced here: 264 us
  Pallas kernels  252 us (95%)
  other arithmetic  6.1 us (2%)
  matrix products  4.37 us (2%)
    pallas_call x1, Pallas kernels, fused(): pl.pallas_call(functools.partial(fused_kernel, dims + (lax.axis_size('pip...  252 us

profile of v1, /device:TPU:0, one launch (start us, length us, event | category | flops | bytes accessed | tf_op | source)
XLA Modules:
  0.0 264.3 jit_solution(15522735232718774102)
XLA Ops:
  0.6 0.0 copy-start
  0.6 0.0 copy-start.6
  0.7 0.0 copy-start.2
  0.7 0.0 copy-start.8
  0.7 1.3 fusion.14
  2.0 0.7 fusion.36
  2.7 0.1 copy.18
  2.8 1.5 fusion.40
  4.3 0.0 copy-done.2
  4.3 0.2 fusion.21
  4.5 0.0 copy-done.8
  4.6 0.1 copy.16
  4.7 0.0 copy-done.6
  4.7 0.4 fusion.41
  5.1 0.1 broadcast_divide_fusion
  5.2 0.7 select_maximum_fusion.refs_3_
  5.9 0.0 copy-done
  5.9 1.1 fusion.15
  7.0 252.1 %shard_map.103 = (f32[2,64,3584]{2,1,0:T(8,128)}, f32[16,512]{1,0:T(8,128)}, f32[1,3584]{1,0:T(1,128)}) custom-call(bf16[64,3584]{1,0:T(8,128)(2,1)} %get-tuple-element.21.refs_0_, bf16[64,3584]{1,0:T(8,128)(2,1)} %get-tuple-element.20.refs_1_, bf16[64,3584]{1,0:T(8,128)(2,1)} %bitcast.70, f32[64,128]{1,0:T(8,128)} %select_maximum_fusion.refs_3_, ...), custom_call_target="tpu_custom_call" | custom-call | tf_op jit(solution)/shard_map/pallas_call | solution.py:880
  259.2 0.0 copy-start.1
  259.2 0.0 copy-start.5
  259.2 0.0 copy-start.3
  259.2 0.0 copy-start.4
  259.2 2.4 fusion.19
  261.7 0.0 copy-done.1
  261.7 0.0 copy-done.5
  261.7 0.0 copy-start.7
  261.7 1.1 fusion.29
  262.8 0.0 copy-done.3
  262.8 0.0 copy-done.4
  262.8 0.9 fusion.24
  263.7 0.0 copy-done.7
  263.7 0.6 copy.24
  (4 shorter events, 0.0 us)
Async XLA Ops:
  0.6 5.3 %copy-start = (bf16[1,64,3584]{2,1,0:T(8,128)(2,1)S(1)}, bf16[1,64,3584]{2,1,0:T(8,128)(2,1)}, u32[]{:S(2)}) copy-start(bf16[1,64,3584]{2,1,0:T(8,128)(2,1)} %param.10) | copy-start | bytes 1376260
  0.6 4.0 %copy-start.6 = (bf16[1,16,3584]{2,1,0:T(8,128)(2,1)S(1)}, bf16[1,16,3584]{2,1,0:T(8,128)(2,1)}, u32[]{:S(2)}) copy-start(bf16[1,16,3584]{2,1,0:T(8,128)(2,1)} %param.13) | copy-start | bytes 344068
  0.7 3.7 %copy-start.2 = (bf16[1,64,3584]{2,1,0:T(8,128)(2,1)S(1)}, bf16[1,64,3584]{2,1,0:T(8,128)(2,1)}, u32[]{:S(2)}) copy-start(bf16[1,64,3584]{2,1,0:T(8,128)(2,1)} %param.8) | copy-start | bytes 1376260
  0.7 3.9 %copy-start.8 = (s32[1,64,8]{1,2,0:T(8,128)S(1)}, s32[1,64,8]{1,2,0:T(8,128)}, u32[]{:S(2)}) copy-start(s32[1,64,8]{1,2,0:T(8,128)} %param.9) | copy-start | bytes 6148
  259.2 2.5 copy-start.1
  259.2 2.5 copy-start.5
  259.2 3.6 %copy-start.3 = (bf16[1,64,3584]{2,1,0:T(8,128)(2,1)S(1)}, bf16[1,64,3584]{2,1,0:T(8,128)(2,1)}, u32[]{:S(2)}) copy-start(bf16[1,64,3584]{2,1,0:T(8,128)(2,1)} %param.8) | copy-start | bytes 1376260
  259.2 3.6 %copy-start.4 = (f32[2,64,3584]{2,1,0:T(8,128)S(1)}, f32[2,64,3584]{2,1,0:T(8,128)}, u32[]{:S(2)}) copy-start(f32[2,64,3584]{2,1,0:T(8,128)} %get-tuple-element.6) | copy-start | bytes 5505028
  261.7 2.0 copy-start.7

commit v2 on v1

--- a/solution.py
+++ b/solution.py
@@ -426,24 +426,32 @@
 
 
 def fused_kernel(dims, *refs):
-    planes, tok, depth, width, dc, n_up, n_pipe = dims
-    (a, b, g, tab, wu, wd, out, lg_out, rg_out) = refs[:9]
-    (rows, tabs, wu_b, wd_b, bu, bd, act, pre, back) = refs[9:18]
-    (o_buf, y_buf, t_buf, z_buf, sc_col, sc_own, sc_all, rg_buf, rg_in) = refs[18:27]
-    (own_s, zs, zr, ys, yr, xs, xr, ms, mr, bus, bds) = refs[27:38]
-    (rys, ryr, rzs, rzr, scs, scr, gs, gr) = refs[38:46]
+    planes, tok, depth, width, dc, rc, n_up, ring, n_pipe = dims
+    (hid_a, hid_b, g, routes_a, routes_b, router, wu, wd, out_a, out_b, rg_out) = refs[:11]
+    (rows, tabs, wu_b, wd_b, bu, bd, act, pre, back, silu, inner) = refs[11:22]
+    (o_buf, y_buf, t_buf, z_buf, f_buf, sc_col, sc_own, sc_all, rg_buf, rg_in) = refs[22:32]
+    (router_t, rinv_b, lifted) = refs[32:35]
+    (own_s, zs, zr, ys, yr, xs, xr, ms, mr, bus, bds) = refs[35:46]
+    (rys, ryr, rzs, rzr, rfs, scs, scr, gs, gr) = refs[46:55]
     slots = 2 * planes
+    experts = 2 * slots
     m_rows = slots * tok
     chunks = depth // dc
     half_d = depth // 2
     half_f = width // 2
+    half_t = tok // 2
     up_rows = half_d // n_up
     tile = 256
+    lanes = tabs.shape[-1]
     me, z, y, x, x_near, y_near = place()
     p = lax.axis_index("pipe")
     mirror = n_pipe - 1 - p
     part = (2 * p) // n_pipe
     slot_me = y * planes + z
+    pair = z + 1 - 2 * (z % 2)
+    opposite = (z + 2) % planes
+    other = (pair + 2) % planes
+    middle = (z + 1) // 2 == 1
 
     def copy(src, dst, send, recv, expert, pipe=p):
         return pltpu.make_async_remote_copy(
@@ -473,6 +481,55 @@
     hello(p, x_near)
     hello(mirror, me)
     hello(mirror, x_near)
+
+    own_g = pltpu.make_async_copy(g, rows.at[2, slot_me], own_s.at[0])
+    own_g.start()
+
+    def nn(lhs, rhs):
+        return jnp.dot(lhs, rhs, preferred_element_type=jnp.float32)
+
+    def nt(lhs, rhs):
+        return lax.dot_general(
+            lhs, rhs, (((1,), (1,)), ((), ())), preferred_element_type=jnp.float32
+        )
+
+    def normalize(k, src):
+        step = 16
+
+        def body(i, carry):
+            r = pl.ds(pl.multiple_of(i * step, step), step)
+            h = src[r, :].astype(jnp.float32)
+            rinv = lax.rsqrt(jnp.mean(h * h, axis=-1, keepdims=True) + EPSILON)
+            rows[k, slot_me, r, :] = (h * rinv).astype(rows.dtype)
+            if k == 1:
+                rinv_b[r, :] = jnp.broadcast_to(rinv, (step, lanes))
+            return carry
+
+        lax.fori_loop(0, tok // step, body, 0)
+
+    normalize(0, hid_a)
+    normalize(1, hid_b)
+    for i in range(3):
+        router_t[i * experts : (i + 1) * experts] = router[...]
+    router_t[3 * experts :] = jnp.zeros((lanes - 3 * experts, depth), router_t.dtype)
+    lane = lax.broadcasted_iota(jnp.int32, (tok, lanes), 1)
+    expert_lane = lax.rem(lane, experts)
+
+    def affinity(k, routes, section):
+        logits = nt(rows[k, slot_me], router_t[...])
+        named = routes[...]
+        chosen = expert_lane == named[:, 0:1]
+        for i in range(1, named.shape[1]):
+            chosen = jnp.logical_or(chosen, expert_lane == named[:, i : i + 1])
+        sig = jnp.where(chosen, jax.nn.sigmoid(logits), 0.0)
+        here = jnp.where(lax.div(lane, experts) == section, sig, 0.0)
+        return sig, here, jnp.sum(here, axis=-1, keepdims=True)
+
+    _, here_a, total_a = affinity(0, routes_a, 0)
+    sig_b, here_b, total_b = affinity(1, routes_b, 1)
+    slope_b = jnp.where(lax.div(lane, experts) == 2, sig_b * (1.0 - sig_b), 0.0)
+    tabs[slot_me] = here_a / total_a + here_b / total_b + slope_b / total_b
+
     pl.semaphore_wait(barrier, slots - 1 + 3)
 
     def up_region(which, i):
@@ -491,6 +548,9 @@
 
     def columns(c):
         return pl.ds(pl.multiple_of(c * dc, dc), dc)
+
+    def fine_columns(c):
+        return pl.ds(pl.multiple_of(c * rc, rc), rc)
 
     def down_x(c):
         r = down_rows(part)
@@ -506,69 +566,109 @@
     for c in range(chunks):
         down_x(c).start()
 
-    ins = [tab, a, b, g]
     bufs = [tabs, rows.at[0], rows.at[1], rows.at[2]]
 
-    def z_copy(k, d, slot):
-        target = chip((z + d) % planes, y)
-        return copy(ins[k], bufs[k].at[slot], zs.at[k, d - 1], zr.at[k, d - 1], target)
-
-    def y_copy(k, d, row):
-        ref = bufs[k].at[row * planes + (z - d + planes) % planes]
-        src = ins[k] if isinstance(d, int) and d == 0 else ref
-        return copy(src, ref, ys.at[k, d], yr.at[k, d], y_near)
-
-    if planes == 4:
-        low, top = (3 - z) // 3, z // 3
-        sources = [1 + 2 * low, 3 - low - top, 2 - low + top]
-        targets = [1 + 2 * top, 3 - low - top, 2 + low - top]
-    else:
-        sources = targets = list(range(1, planes))
+    def block(k, row, source):
+        return bufs[k].at[row * planes + source]
+
+    def mine(k):
+        return g if k == 3 else bufs[k].at[slot_me]
+
+    def z_send(k, target):
+        dst = bufs[k].at[slot_me]
+        return copy(mine(k), dst, zs.at[k, target], zr.at[k, z], chip(target, y))
+
+    def z_take(k, source):
+        ref = block(k, y, source)
+        return copy(ref, ref, zs.at[k, source], zr.at[k, source], chip(source, y))
+
+    def z_relay(k):
+        ref = block(k, y, opposite)
+        return copy(ref, ref, zs.at[k, z], zr.at[k, opposite], chip(pair, y))
+
+    def late(ref):
+        return ref.at[pl.ds(half_t, half_t)]
+
+    def early(ref):
+        return ref.at[pl.ds(0, half_t)]
+
+    def cross(k, source):
+        ref = late(block(k, 1 - y, source))
+        return copy(ref, ref, zs.at[k, planes], zr.at[k, planes], chip(pair, y))
+
+    def y_send(k):
+        return copy(mine(k), bufs[k].at[slot_me], ys.at[k, z], yr.at[k, z], y_near)
+
+    def y_copy(k, source, row):
+        ref = block(k, row, source)
+        return copy(ref, ref, ys.at[k, source], yr.at[k, source], y_near)
+
+    def y_half(k, row):
+        ref = early(block(k, row, pair))
+        return copy(ref, ref, ys.at[k, pair], yr.at[k, pair], y_near)
+
+    def spread(k):
+        y_send(k).start()
+        z_send(k, pair).start()
+
+        @pl.when(middle)
+        def _():
+            z_send(k, other).start()
+
+        z_send(k, opposite).start()
 
     def serve(k, i):
-        d = sources[i]
-        z_copy(k, d, y * planes + (z - d + planes) % planes).wait_recv()
-        y_copy(k, d, y).start()
+        if i == 0:
+            z_take(k, pair).wait_recv()
+            y_half(k, y).start()
+            y_copy(k, z, 1 - y).wait_recv()
+            cross(k, z).start()
+        if i == 1:
+            z_take(k, opposite).wait_recv()
+
+            @pl.when(middle)
+            def _():
+                z_relay(k).start()
+
+            y_copy(k, opposite, y).start()
+        if i == 2:
+            z_take(k, other).wait_recv()
+            y_copy(k, other, y).start()
 
     def arrived(k):
-        for d in range(planes):
-            y_copy(k, d, 1 - y).wait_recv()
+        y_half(k, 1 - y).wait_recv()
+        y_copy(k, opposite, 1 - y).wait_recv()
+        y_copy(k, other, 1 - y).wait_recv()
+        cross(k, pair).wait_recv()
 
     for k in range(4):
-        y_copy(k, 0, y).start()
-        for d in targets:
-            z_copy(k, d, slot_me).start()
-    own = [pltpu.make_async_copy(ins[k], bufs[k].at[slot_me], own_s.at[k]) for k in range(4)]
-    for k in range(4):
-        own[k].start()
+        spread(k)
 
     def chunk_of(k, c):
         return rows[k, :, :, columns(c)].reshape(m_rows, dc)
 
-    def nn(lhs, rhs):
-        return jnp.dot(lhs, rhs, preferred_element_type=jnp.float32)
-
-    def nt(lhs, rhs):
-        return lax.dot_general(
-            lhs, rhs, (((1,), (1,)), ((), ())), preferred_element_type=jnp.float32
-        )
-
     def load_up(c):
         return pltpu.make_async_copy(wu.at[columns(c)], bu.at[c % 2], bus.at[c % 2])
 
+    def load_fine(c):
+        return pltpu.make_async_copy(wu.at[fine_columns(c)], bu.at[c % 2, :rc], bus.at[c % 2])
+
     def load_down(c):
         return pltpu.make_async_copy(wd.at[:, columns(c)], bd.at[c % 2], bds.at[c % 2])
 
-    def next_chunk(load, c):
+    def next_chunk(load, c, count=chunks):
         load(c).wait()
 
-        @pl.when(c + 1 < chunks)
+        @pl.when(c + 1 < count)
         def _():
             load(c + 1).start()
+
+    def block_rows(s):
+        return pl.ds(pl.multiple_of(s * tok, tok), tok)
 
     def clear(dst):
         def body(s, carry):
-            dst[pl.ds(pl.multiple_of(s * tok, tok), tok), :] = jnp.zeros((tok, width), jnp.float32)
+            dst[block_rows(s), :] = jnp.zeros((tok, width), jnp.float32)
             return carry
 
         lax.fori_loop(0, slots, body, 0)
@@ -590,87 +690,153 @@
 
         lax.fori_loop(0, chunks, body, 0)
 
-    lane = lax.broadcasted_iota(jnp.int32, (tok, tabs.shape[-1]), 1)
-
     def pick(s, column):
         return jnp.sum(jnp.where(lane == column, tabs[s], 0.0), axis=-1, keepdims=True)
 
-    experts = 2 * slots
     expert_of = [me, x_near]
 
     def activate(which, src):
         def body(s, carry):
-            r = pl.ds(pl.multiple_of(s * tok, tok), tok)
-            v = src[r, :]
-            act[which, r, :] = (v * jax.nn.sigmoid(v) * pick(s, expert_of[which])).astype(act.dtype)
+            v = src[block_rows(s), :]
+            weight = pick(s, expert_of[which])
+            act[which, block_rows(s), :] = (v * jax.nn.sigmoid(v) * weight).astype(act.dtype)
             return carry
 
         lax.fori_loop(0, slots, body, 0)
 
-    def invert():
+    def prepare_b(which):
         def body(s, carry):
-            r = pl.ds(pl.multiple_of(s * tok, tok), tok)
-            scores = []
-            for which in range(2):
-                v = pre[which, r, :]
-                bk = back[which, r, :]
-                sig = jax.nn.sigmoid(v)
-                scores.append(jnp.sum(bk * (v * sig), axis=-1, keepdims=True))
-                inner = bk * (sig * (1.0 + v * (1.0 - sig)))
-                weight = pick(s, experts + expert_of[which])
-                act[which, r, :] = (inner * weight).astype(act.dtype)
-            even = jnp.where(x == 0, scores[0], scores[1])
-            odd = jnp.where(x == 0, scores[1], scores[0])
-            sc_col[s] = jnp.where(lane == 0, even, jnp.where(lane == 1, odd, 0.0))
+            r = block_rows(s)
+            v = pre[which, r, :]
+            sig = jax.nn.sigmoid(v)
+            silu[which, r, :] = (v * sig).astype(silu.dtype)
+            weight = pick(s, experts + expert_of[which])
+            pre[which, r, :] = sig * (1.0 + v * (1.0 - sig)) * weight
             return carry
 
         lax.fori_loop(0, slots, body, 0)
-        sc_own[...] = sc_col[...].reshape(m_rows, lane.shape[1]).T[:8]
-
-    steps = 2 * chunks
+
+    def invert(which):
+        def body(s, carry):
+            r = block_rows(s)
+            bk = back[which, r, :]
+            score = jnp.sum(bk * silu[which, r, :].astype(jnp.float32), axis=-1, keepdims=True)
+            inner[which, r, :] = (bk * pre[which, r, :]).astype(inner.dtype)
+            at = x if which == 0 else 1 - x
+            held = 0.0 if which == 0 else sc_col[s]
+            sc_col[s] = jnp.where(lane == at, score, held)
+            return carry
+
+        lax.fori_loop(0, slots, body, 0)
+
+    fine = depth // rc
+    steps = 2 * fine
 
     def rs_y(q):
-        src = o_buf.at[q, pl.ds((1 - y) * planes, planes)]
+        src = o_buf.at[q % ring, pl.ds((1 - y) * planes, planes)]
         return copy(src, y_buf.at[q], rys.at[q], ryr.at[q], y_near)
 
-    def rs_z(q, d):
-        plane = (z + d) % planes
-        src = t_buf.at[q, plane]
-        return copy(src, z_buf.at[q, d - 1], rzs.at[q, d - 1], rzr.at[q, d - 1], chip(plane, y))
+    def rs_z(q, target, place_at):
+        src = t_buf.at[q % ring, target]
+        return copy(src, z_buf.at[q, place_at], rzs.at[q], rzr.at[q], chip(target, y))
+
+    def rs_far(q):
+        src = t_buf.at[q % ring, other]
+        return copy(src, f_buf.at[q], rzs.at[q], rfs.at[q], chip(pair, y))
+
+    def sent_z(q):
+        src = t_buf.at[q % ring, pl.ds(0, planes - 1)]
+        dst = z_buf.at[q, pl.ds(0, planes - 1)]
+        copy(src, dst, rzs.at[q], rzr.at[q], chip(pair, y)).wait_send()
 
     def fold_y(q):
         rs_y(q).wait_recv()
+
+        def clean():
+            sent_z(q - ring)
+
+        if isinstance(q, int):
+            if q >= ring:
+                clean()
+        else:
+            pl.when(q >= ring)(clean)
         for k in range(planes):
-            both = o_buf[q, y * planes + k].astype(jnp.float32) + y_buf[q, k].astype(jnp.float32)
-            t_buf[q, k] = both.astype(t_buf.dtype)
-        for d in targets:
-            rs_z(q, d).start()
+            first = o_buf[q % ring, y * planes + k].astype(jnp.float32)
+            t_buf[q % ring, k] = (first + y_buf[q, k].astype(jnp.float32)).astype(t_buf.dtype)
+        rs_z(q, pair, 0).start()
+
+        @pl.when(middle)
+        def _():
+            rs_z(q, other, 2).start()
+
+        @pl.when(jnp.logical_not(middle))
+        def _():
+            rs_far(q).start()
+            rs_z(q, opposite, 1).start()
+
+    def relay_z(q):
+        @pl.when(middle)
+        def _():
+            rs_far(q).wait_recv()
+            total = t_buf[q % ring, opposite].astype(jnp.float32) + f_buf[q].astype(jnp.float32)
+            t_buf[q % ring, opposite] = total.astype(t_buf.dtype)
+            rs_z(q, opposite, 1).start()
+
+    def take_z(q, count):
+        src = t_buf.at[q % ring, pl.ds(0, count)]
+        dst = z_buf.at[q, pl.ds(0, count)]
+        copy(src, dst, rzs.at[q], rzr.at[q], chip(pair, y)).wait_recv()
+        total = t_buf[q % ring, z].astype(jnp.float32)
+        for i in range(count):
+            total = total + z_buf[q, i].astype(jnp.float32)
+        return total
 
     def fold_z(q):
-        total = t_buf[q, z].astype(jnp.float32)
-        for d in range(1, planes):
-            rs_z(q, d).wait_recv()
-            total = total + z_buf[q, d - 1].astype(jnp.float32)
-        out[q // chunks, :, columns(q % chunks)] = total
+        def settle(total):
+            def of_a():
+                cols = fine_columns(q)
+                mixed = hid_a[:, cols].astype(jnp.float32) + ROUTED_SCALE * total
+                out_a[:, cols] = mixed.astype(out_a.dtype)
+
+            def of_b():
+                lifted[:, fine_columns(q - fine)] = total
+
+            if isinstance(q, int):
+                of_a() if q < fine else of_b()
+            else:
+                pl.when(q < fine)(of_a)
+                pl.when(q >= fine)(of_b)
+
+        @pl.when(middle)
+        def _():
+            settle(take_z(q, planes - 1))
+
+        @pl.when(jnp.logical_not(middle))
+        def _():
+            settle(take_z(q, planes - 2))
+
+    lags = ((2, fold_y), (4, relay_z), (6, fold_z))
 
     def behind(q):
-        @pl.when(q >= 2)
-        def _():
-            fold_y(q - 2)
-
-        @pl.when(q >= 4)
-        def _():
-            fold_z(q - 4)
-
-    def store(q, n, value):
-        cols = pl.ds(n * tile, tile)
-        o_buf[q, :, :, cols] = value.reshape(slots, tok, tile).astype(o_buf.dtype)
+        for lag, stage in lags:
+            if isinstance(q, int):
+                if lag <= q < steps + lag:
+                    stage(q - lag)
+            else:
+                pl.when(q >= lag)(functools.partial(stage, q - lag))
+
+    def store(q, value):
+        def clean():
+            rs_y(q - ring).wait_send()
+
+        pl.when(q >= ring)(clean)
+        o_buf[q % ring] = value.reshape(slots, tok, rc).astype(o_buf.dtype)
+        rs_y(q).start()
 
     for k in range(3):
-        for i in range(planes - 1):
+        for i in range(3):
             serve(k, i)
-    for k in range(4):
-        own[k].wait()
+    own_g.wait()
     arrived(0)
     arrived(1)
     project(0, False, back.at[0])
@@ -683,16 +849,17 @@
         up_m(i, 1 - part).wait_recv()
     project(0, True, back.at[1])
     activate(1, back.at[1])
-    for i in range(1, planes - 2):
-        serve(3, i)
+    serve(3, 1)
     arrived(2)
     project(1, False, pre.at[0])
-    for i in range(max(1, planes - 2), planes - 1):
-        serve(3, i)
+    prepare_b(0)
+    serve(3, 2)
     project(1, True, pre.at[1])
+    prepare_b(1)
     clear(back.at[0])
     clear(back.at[1])
     load_down(0).start()
+    load_fine(0).start()
     down_x(0).wait_recv()
     down_m(0, part).start()
     arrived(3)
@@ -700,52 +867,67 @@
     def forward(c, carry):
         next_chunk(load_down, c)
         down_m(c, 1 - part).wait_recv()
-        for n in range(dc // tile):
+        for n in range(dc // rc):
+            cols = pl.ds(n * rc, rc)
+            value = nn(act[0], bd[c % 2, :, cols]) + nn(act[1], wd_b[c, :, cols])
+            store(c * (dc // rc) + n, value)
+        lhs = chunk_of(2, c)
+        for n in range(width // tile):
             cols = pl.ds(n * tile, tile)
-            store(c, n, nn(act[0], bd[c % 2, :, cols]) + nn(act[1], wd_b[c, :, cols]))
-        rs_y(c).start()
+            back[1, :, cols] += nt(lhs, wd_b[c, cols, :])
+
+        @pl.when(c + 1 < chunks)
+        def _():
+            down_x(c + 1).wait_recv()
+            down_m(c + 1, part).start()
+
+        for n in range(dc // rc):
+            behind(c * (dc // rc) + n)
+        return carry
+
+    def own_back(c, carry):
+        next_chunk(load_down, c)
         lhs = chunk_of(2, c)
         for n in range(width // tile):
             cols = pl.ds(n * tile, tile)
             back[0, :, cols] += nt(lhs, bd[c % 2, cols, :])
-            back[1, :, cols] += nt(lhs, wd_b[c, cols, :])
-
-        @pl.when(c + 1 < chunks)
-        def _():
-            down_x(c + 1).wait_recv()
-            down_m(c + 1, part).start()
-
-        behind(c)
         return carry
 
-    lax.fori_loop(0, chunks, forward, 0)
-    load_up(0).start()
-    invert()
+    first = min(4, chunks - 1)
+    lax.fori_loop(0, first, forward, 0)
+    load_down(first).wait()
+    load_down(0).start()
+    lax.fori_loop(0, chunks, own_back, 0)
+    invert(0)
+    load_down(first).start()
+    lax.fori_loop(first, chunks, forward, 0)
+    invert(1)
 
     def score_copy(i, slot):
         target = of_slot((slot_me + i) % slots)
         return copy(sc_own, sc_all.at[slot], scs.at[i - 1], scr.at[i - 1], target)
 
-    for i in range(1, slots):
-        score_copy(i, slot_me).start()
-
     def backward(c, carry):
-        next_chunk(load_up, c)
-        q = chunks + c
-        for n in range(dc // tile):
-            cols = pl.ds(n * tile, tile)
-            shared = pl.ds(pl.multiple_of(c * dc + n * tile, tile), tile)
-            store(q, n, nt(act[0], bu[c % 2, cols, :]) + nt(act[1], wu_b[shared, :]))
-        rs_y(q).start()
+        next_chunk(load_fine, c, fine)
+        q = fine + c
+        value = nt(inner[0], bu[c % 2, :rc, :]) + nt(inner[1], wu_b[fine_columns(c), :])
+        store(q, value)
         behind(q)
+
+        @pl.when(c == 1)
+        def _():
+            sc_own[...] = sc_col[...].reshape(m_rows, lanes).T[:8]
+            for i in range(1, slots):
+                score_copy(i, slot_me).start()
+
         return carry
 
-    lax.fori_loop(0, chunks, backward, 0)
+    lax.fori_loop(0, fine, backward, 0)
 
     sc_all[slot_me] = sc_own[...]
     for i in range(1, slots):
         score_copy(i, (slot_me - i + slots) % slots).wait_recv()
-    table = tabs[...].reshape(m_rows, lane.shape[1]).T
+    table = tabs[...].reshape(m_rows, lanes).T
     lines = []
     for e in range(experts):
         plane, row, odd = e // PLANE, (e // 2) % 2, e % 2
@@ -754,19 +936,22 @@
     gate = ROUTED_SCALE * score
     mean = jnp.sum(gate * table[experts : 2 * experts], axis=0, keepdims=True)
     logit = table[2 * experts : 3 * experts] * (gate - mean)
-    lg_out[...] = logit
     order = lax.broadcasted_iota(jnp.int32, (experts, m_rows), 0)
-    mine = jnp.sum(jnp.where(order == me, logit, 0.0), axis=0, keepdims=True)
-    theirs = jnp.sum(jnp.where(order == x_near, logit, 0.0), axis=0, keepdims=True)
-    both = jnp.concatenate([mine, theirs, jnp.zeros((6, m_rows), jnp.float32)], axis=0)
-    high = both.astype(jnp.bfloat16)
-    rest = both - high.astype(jnp.float32)
-    middle = rest.astype(jnp.bfloat16)
-    last = (rest - middle.astype(jnp.float32)).astype(jnp.bfloat16)
+    one = jnp.sum(jnp.where(order == me, logit, 0.0), axis=0, keepdims=True)
+    two = jnp.sum(jnp.where(order == x_near, logit, 0.0), axis=0, keepdims=True)
+    both = jnp.concatenate([one, two, jnp.zeros((6, m_rows), jnp.float32)], axis=0)
+
+    def thirds(v):
+        high = v.astype(jnp.bfloat16)
+        rest = v - high.astype(jnp.float32)
+        medium = rest.astype(jnp.bfloat16)
+        return (high, medium, (rest - medium.astype(jnp.float32)).astype(jnp.bfloat16))
+
+    pieces = thirds(both)
     for c in range(chunks):
         cols = pl.ds(c * dc, dc)
         rhs = rows[1, :, :, cols].reshape(m_rows, dc)
-        rg_buf[:, cols] = nn(high, rhs) + nn(middle, rhs) + nn(last, rhs)
+        rg_buf[:, cols] = nn(pieces[0], rhs) + nn(pieces[1], rhs) + nn(pieces[2], rhs)
 
     def grad_copy(i):
         expert = me if i == 0 else x_near
@@ -775,20 +960,47 @@
 
     for i in range(3):
         grad_copy(i).start()
-    for q in range(steps - 2, steps):
-        fold_y(q)
-        fold_z(q - 2)
+    padded = jnp.concatenate([logit, jnp.zeros((lanes - experts, m_rows), jnp.float32)], axis=0)
+    sc_col[...] = padded.T.reshape(slots, tok, lanes)
+    for q in range(steps, steps + 3):
+        behind(q)
+    dense = thirds(sc_col[slot_me])
+    for q in range(steps + 3, steps + lags[-1][0]):
+        behind(q)
+
+    inv = rinv_b[:, 0:1]
+    dots = jnp.zeros((tok, 1), jnp.float32)
+    for c in range(chunks):
+        cols = pl.ds(c * dc, dc)
+        rhs = router_t[:, cols]
+        extra = nn(dense[0], rhs) + nn(dense[1], rhs) + nn(dense[2], rhs)
+        v = ROUTED_SCALE * lifted[:, cols] + extra
+        lifted[:, cols] = v
+        dots = dots + jnp.sum(v * hid_b[:, cols].astype(jnp.float32), axis=-1, keepdims=True)
+    slope = inv * inv * inv * (dots / depth)
+    for c in range(chunks):
+        cols = pl.ds(c * dc, dc)
+        grad = g[:, cols].astype(jnp.float32) + inv * lifted[:, cols]
+        grad = grad - hid_b[:, cols].astype(jnp.float32) * slope
+        out_b[:, cols] = grad.astype(out_b.dtype)
     for i in range(3):
         grad_copy(i).wait_recv()
     rg_out[...] = rg_buf[0:1, :] + rg_in[0, 0:1, :] + rg_in[1, 1:2, :] + rg_in[2, 1:2, :]
-    for q in range(steps - 2, steps):
-        fold_z(q)
 
     for k in range(4):
-        for d in range(1, planes):
-            z_copy(k, d, slot_me).wait_send()
-        for d in range(planes):
-            y_copy(k, d, y).wait_send()
+        z_send(k, pair).wait_send()
+        z_send(k, opposite).wait_send()
+
+        @pl.when(middle)
+        def _():
+            z_send(k, other).wait_send()
+            z_relay(k).wait_send()
+
+        cross(k, z).wait_send()
+        y_send(k).wait_send()
+        y_half(k, y).wait_send()
+        for source in (opposite, other):
+            y_copy(k, source, y).wait_send()
     for i in range(n_up):
         up_x(i).wait_send()
         up_m(i, part).wait_send()
@@ -802,11 +1014,10 @@
 
     def drain_rs(q, carry):
         rs_y(q).wait_send()
-        for d in range(1, planes):
-            rs_z(q, d).wait_send()
+        sent_z(q)
         return carry
 
-    lax.fori_loop(0, steps, drain_rs, 0)
+    lax.fori_loop(steps - ring, steps, drain_rs, 0)
     for i in range(1, slots):
         score_copy(i, slot_me).wait_send()
     for i in range(3):
@@ -814,6 +1025,7 @@
 
 
 N_UP = 4
+RING = 8
 
 
 def fused_plan(n, tok, depth, width):
@@ -821,8 +1033,9 @@
     slots = 2 * planes
     m_rows = slots * tok
     dc = 512 if depth % 512 == 0 else 256
+    rc = 256
     chunks = depth // dc
-    steps = 2 * chunks
+    steps = 2 * (depth // rc)
     bf, f32 = jnp.bfloat16, jnp.float32
     buffers = [
         ((3, slots, tok, depth), bf),
@@ -834,95 +1047,74 @@
         ((2, m_rows, width), bf),
         ((2, m_rows, width), f32),
         ((2, m_rows, width), f32),
-        ((steps, slots, tok, dc), bf),
-        ((steps, planes, tok, dc), bf),
-        ((steps, planes, tok, dc), bf),
-        ((steps, planes - 1, tok, dc), bf),
+        ((2, m_rows, width), bf),
+        ((2, m_rows, width), bf),
+        ((RING, slots, tok, rc), bf),
+        ((steps, planes, tok, rc), bf),
+        ((RING, planes, tok, rc), bf),
+        ((steps, planes - 1, tok, rc), bf),
+        ((steps, tok, rc), bf),
         ((slots, tok, 128), f32),
         ((8, m_rows), f32),
         ((slots, 8, m_rows), f32),
         ((8, depth), f32),
         ((3, 8, depth), f32),
+        ((128, depth), bf),
+        ((tok, 128), f32),
+        ((tok, depth), f32),
     ]
-    sems = [
-        (4,),
-        (4, planes - 1),
-        (4, planes - 1),
-        (4, planes),
-        (4, planes),
-        (N_UP + chunks,),
-        (N_UP + chunks,),
-        (N_UP + chunks,),
-        (N_UP + chunks,),
-        (2,),
-        (2,),
-        (steps,),
-        (steps,),
-        (steps, planes - 1),
-        (steps, planes - 1),
-        (slots - 1,),
-        (slots - 1,),
-        (3,),
-        (3,),
-    ]
+    sems = (
+        [(1,)]
+        + [(4, planes + 1)] * 2
+        + [(4, planes)] * 2
+        + [(N_UP + chunks,)] * 4
+        + [(2,)] * 2
+        + [(steps,)] * 5
+        + [(slots - 1,)] * 2
+        + [(3,)] * 2
+    )
     total = sum(math.prod(shape) * jnp.dtype(kind).itemsize for shape, kind in buffers)
-    outs = 2 * tok * depth * 4 + 3 * tok * depth * 2
-    fits = total + outs < 64_500_000 and 3 * n <= 128
-    return fits, (planes, tok, depth, width, dc, N_UP), buffers, sems
-
-
-def fused(normed_a, normed_b, grad_out, table, up, down, plan):
+    fits = total + 5 * tok * depth * 2 < 64_500_000 and 3 * n <= 128 and planes == 4
+    return fits, (planes, tok, depth, width, dc, rc, N_UP, RING), buffers, sems
+
+
+def fused(plan, *args):
     _, dims, buffers, sems = plan
-    planes, tok, depth = dims[:3]
-    slots = 2 * planes
+    tok, depth = dims[1:3]
     vmem = pl.BlockSpec(memory_space=pltpu.VMEM)
     hbm = pl.BlockSpec(memory_space=pl.ANY)
     return pl.pallas_call(
         functools.partial(fused_kernel, dims + (lax.axis_size("pipe"),)),
         out_shape=[
-            jax.ShapeDtypeStruct((2, tok, depth), jnp.float32),
-            jax.ShapeDtypeStruct((2 * slots, slots * tok), jnp.float32),
+            jax.ShapeDtypeStruct((tok, depth), jnp.bfloat16),
+            jax.ShapeDtypeStruct((tok, depth), jnp.bfloat16),
             jax.ShapeDtypeStruct((1, depth), jnp.float32),
         ],
-        in_specs=[vmem] * 4 + [hbm] * 2,
+        in_specs=[vmem] * 6 + [hbm] * 2,
         out_specs=[vmem] * 3,
         scratch_shapes=[pltpu.VMEM(shape, kind) for shape, kind in buffers]
         + [DMA(shape) for shape in sems],
         compiler_params=pltpu.CompilerParams(
             collective_id=7, has_side_effects=True, vmem_limit_bytes=67_000_000
         ),
-    )(normed_a, normed_b, grad_out, table, up, down)
+    )(*args)
 
 
 def on_device_fused(
     plan, hidden_a, routes_a, hidden_b, routes_b, grad_out_b, router, w_up, w_down
 ):
-    router_segment = router[0]
-    n_expert = router_segment.shape[0]
-    planes, tok = plan[1][:2]
-    hidden32_a, rinv_a, normed_a, affinity_a = prepare(hidden_a[0], routes_a[0], router_segment)
-    hidden32_b, rinv_b, normed_b, affinity_b = prepare(hidden_b[0], routes_b[0], router_segment)
-    grad_out = grad_out_b[0]
-    total_b = jnp.sum(affinity_b, axis=1, keepdims=True)
-    weight_a = affinity_a / jnp.sum(affinity_a, axis=1, keepdims=True)
-    weight_b = affinity_b / total_b
-    slope_b = affinity_b * (1.0 - affinity_b) / total_b
-    table = jnp.concatenate([weight_a, weight_b, slope_b], axis=1)
-    table = jnp.pad(table, ((0, 0), (0, 128 - 3 * n_expert)))
-    sums, logit_grad, router_grad = fused(
-        normed_a, normed_b, grad_out, table, w_up[0, 0], w_down[0, 0], plan
+    outs = fused(
+        plan,
+        hidden_a[0],
+        hidden_b[0],
+        grad_out_b[0],
+        routes_a[0],
+        routes_b[0],
+        router[0],
+        w_up[0, 0],
+        w_down[0, 0],
     )
-    layer_out = (hidden32_a + ROUTED_SCALE * sums[0]).astype(jnp.bfloat16)
-    _, z, y, _, _, _ = place()
-    dense = lax.dynamic_slice_in_dim(logit_grad, (y * planes + z) * tok, tok, axis=1)
-    normed_grad = ROUTED_SCALE * sums[1] + jnp.einsum(
-        "et,ed->td", dense, router_segment.astype(jnp.float32), precision=lax.Precision.HIGHEST
-    )
-    mean_term = jnp.mean(normed_grad * hidden32_b, axis=-1, keepdims=True)
-    grad_in = (
-        grad_out.astype(jnp.float32) + rinv_b * normed_grad - hidden32_b * rinv_b**3 * mean_term
-    )
-    return (layer_out[None], grad_in.astype(jnp.bfloat16)[None], router_grad[None])
+    return tuple(o[None] for o in outs)
 
 
 def solution(mesh):

time: 265 us -> 253 us (0.955)
  Pallas kernels: 252 us -> 244 us
  local copies, waits for them, and re-layouts: 0.84 us -> 7.71 us
  other arithmetic: 6.1 us -> 0 us
  matrix products: 4.37 us -> 0 us
    pallas_call x1, Pallas kernels: 252 us -> 244 us  [fused(): pl.pallas_call(functools.partial(fused_kernel, dims + (lax.axis_size('pip...]
    unnamed x19 -> x5, local copies, waits for them, and re-layouts: 0.65 us -> 7.71 us
    dot_general x3 -> x0, matrix products: 4.37 us -> none  [the longest x1 2.45 us: on_device_fused(): jnp.einsum('et,ed->td', dense, router_segment.astype(jnp.float32), precis...]
where the time goes in v2:
time: 253 us; the launch traced here: 252 us
  Pallas kernels  244 us (96%)
  local copies, waits for them, and re-layouts  7.71 us (3%)
    pallas_call x1, Pallas kernels, fused(): pl.pallas_call(functools.partial(fused_kernel, dims + (lax.axis_size('pip...  244 us
    unnamed x5, local copies, waits for them, and re-layouts  7.71 us

profile of v2, /device:TPU:0, one launch (start us, length us, event | category | flops | bytes accessed | tf_op | source)
XLA Modules:
  0.0 252.2 jit_solution(17014697593126057545)
XLA Ops:
  0.6 1.4 copy.11
  2.0 1.4 copy.12
  3.4 243.9 %shard_map.103 = (bf16[64,3584]{1,0:T(8,128)(2,1)}, bf16[64,3584]{1,0:T(8,128)(2,1)}, f32[1,3584]{1,0:T(1,128)}) custom-call(bf16[64,3584]{1,0:T(8,128)(2,1)} %bitcast.15, bf16[64,3584]{1,0:T(8,128)(2,1)} %bitcast.16, bf16[64,3584]{1,0:T(8,128)(2,1)} %bitcast.17, s32[64,8]{1,0:T(8,128)} %bitcast.18, s32[64,8]{1,0:T(8,128)} %bitcast.19, ...), custom_call_target="tpu_custom_call" | custom-call | tf_op jit(solution)/shard_map/pallas_call | solution.py:1086
  247.3 1.8 copy.16
  249.1 1.8 copy.17
  250.9 1.3 copy.18

commit v3 on v2

--- a/solution.py
+++ b/solution.py
@@ -517,7 +517,7 @@
 
     def affinity(k, routes, section):
         logits = nt(rows[k, slot_me], router_t[...])
-        named = routes[...]
+        named = routes[...].T
         chosen = expert_lane == named[:, 0:1]
         for i in range(1, named.shape[1]):
             chosen = jnp.logical_or(chosen, expert_lane == named[:, i : i + 1])
@@ -609,26 +609,39 @@
 
     def spread(k):
         y_send(k).start()
-        z_send(k, pair).start()
 
         @pl.when(middle)
         def _():
+            if k < 2:
+                z_send(k, pair).start()
             z_send(k, other).start()
+
+        @pl.when(jnp.logical_not(middle))
+        def _():
+            z_send(k, pair).start()
+            if k == 0:
+                z_send(k, other).start()
 
         z_send(k, opposite).start()
 
     def serve(k, i):
         if i == 0:
             z_take(k, pair).wait_recv()
-            y_half(k, y).start()
-            y_copy(k, z, 1 - y).wait_recv()
-            cross(k, z).start()
+            if k < 2:
+                y_copy(k, pair, y).start()
+            else:
+                y_half(k, y).start()
+                y_copy(k, z, 1 - y).wait_recv()
+                cross(k, z).start()
         if i == 1:
             z_take(k, opposite).wait_recv()
 
             @pl.when(middle)
             def _():
-                z_relay(k).start()
+                if k > 0:
+                    z_relay(k).start()
+                if 0 < k < 3:
+                    z_send(k + 1, pair).start()
 
             y_copy(k, opposite, y).start()
         if i == 2:
@@ -636,10 +649,14 @@
             y_copy(k, other, y).start()
 
     def arrived(k):
-        y_half(k, 1 - y).wait_recv()
+        if k < 2:
+            y_copy(k, z, 1 - y).wait_recv()
+            y_copy(k, pair, 1 - y).wait_recv()
+        else:
+            y_half(k, 1 - y).wait_recv()
+            cross(k, pair).wait_recv()
         y_copy(k, opposite, 1 - y).wait_recv()
         y_copy(k, other, 1 - y).wait_recv()
-        cross(k, pair).wait_recv()
 
     for k in range(4):
         spread(k)
@@ -647,21 +664,44 @@
     def chunk_of(k, c):
         return rows[k, :, :, columns(c)].reshape(m_rows, dc)
 
+    class Pieces:
+        def __init__(self, src, dst, sem):
+            self.whole = pltpu.make_async_copy(src, dst, sem)
+            count = 4
+            step = dst.shape[0] // count
+            self.parts = [
+                pltpu.make_async_copy(src.at[r], dst.at[r], sem)
+                for r in (pl.ds(i * step, step) for i in range(count))
+            ]
+
+        def start(self):
+            for part_copy in self.parts:
+                part_copy.start()
+
+        def wait(self):
+            self.whole.wait()
+
+    depth_of = bu.shape[0]
+
     def load_up(c):
-        return pltpu.make_async_copy(wu.at[columns(c)], bu.at[c % 2], bus.at[c % 2])
+        return Pieces(wu.at[columns(c)], bu.at[c % depth_of], bus.at[c % depth_of])
 
     def load_fine(c):
-        return pltpu.make_async_copy(wu.at[fine_columns(c)], bu.at[c % 2, :rc], bus.at[c % 2])
+        return Pieces(wu.at[fine_columns(c)], bu.at[c % depth_of, pl.ds(0, rc)], bus.at[c % depth_of])
 
     def load_down(c):
-        return pltpu.make_async_copy(wd.at[:, columns(c)], bd.at[c % 2], bds.at[c % 2])
+        return Pieces(wd.at[:, columns(c)], bd.at[c % depth_of], bds.at[c % depth_of])
+
+    def prime(load, lo, hi):
+        for c in range(lo, min(hi, lo + depth_of - 1)):
+            load(c).start()
 
     def next_chunk(load, c, count=chunks):
         load(c).wait()
 
-        @pl.when(c + 1 < count)
-        def _():
-            load(c + 1).start()
+        @pl.when(c + depth_of - 1 < count)
+        def _():
+            load(c + depth_of - 1).start()
 
     def block_rows(s):
         return pl.ds(pl.multiple_of(s * tok, tok), tok)
@@ -676,7 +716,7 @@
     def project(k, partner, dst):
         clear(dst)
         if not partner:
-            load_up(0).start()
+            prime(load_up, 0, chunks)
 
         def body(c, carry):
             if not partner:
@@ -684,7 +724,7 @@
             lhs = chunk_of(k, c)
             for n in range(width // tile):
                 cols = pl.ds(n * tile, tile)
-                rhs = wu_b[columns(c), cols] if partner else bu[c % 2, :, cols]
+                rhs = wu_b[columns(c), cols] if partner else bu[c % depth_of, :, cols]
                 dst[:, cols] += nn(lhs, rhs)
             return carry
 
@@ -794,9 +834,7 @@
     def fold_z(q):
         def settle(total):
             def of_a():
-                cols = fine_columns(q)
-                mixed = hid_a[:, cols].astype(jnp.float32) + ROUTED_SCALE * total
-                out_a[:, cols] = mixed.astype(out_a.dtype)
+                out_a[:, fine_columns(q)] = ROUTED_SCALE * total
 
             def of_b():
                 lifted[:, fine_columns(q - fine)] = total
@@ -815,7 +853,7 @@
         def _():
             settle(take_z(q, planes - 2))
 
-    lags = ((2, fold_y), (4, relay_z), (6, fold_z))
+    lags = ((4, fold_y), (6, relay_z), (8, fold_z))
 
     def behind(q):
         for lag, stage in lags:
@@ -833,74 +871,116 @@
         o_buf[q % ring] = value.reshape(slots, tok, rc).astype(o_buf.dtype)
         rs_y(q).start()
 
-    for k in range(3):
-        for i in range(3):
-            serve(k, i)
-    own_g.wait()
-    arrived(0)
-    arrived(1)
-    project(0, False, back.at[0])
-    activate(0, back.at[0])
-    serve(3, 0)
-    for i in range(n_up):
+    def take_up(i):
         up_x(i).wait_recv()
         up_m(i, part).start()
-    for i in range(n_up):
-        up_m(i, 1 - part).wait_recv()
-    project(0, True, back.at[1])
-    activate(1, back.at[1])
-    serve(3, 1)
-    arrived(2)
-    project(1, False, pre.at[0])
-    prepare_b(0)
-    serve(3, 2)
-    project(1, True, pre.at[1])
-    prepare_b(1)
-    clear(back.at[0])
-    clear(back.at[1])
-    load_down(0).start()
-    load_fine(0).start()
-    down_x(0).wait_recv()
-    down_m(0, part).start()
-    arrived(3)
-
-    def forward(c, carry):
-        next_chunk(load_down, c)
-        down_m(c, 1 - part).wait_recv()
-        for n in range(dc // rc):
-            cols = pl.ds(n * rc, rc)
-            value = nn(act[0], bd[c % 2, :, cols]) + nn(act[1], wd_b[c, :, cols])
-            store(c * (dc // rc) + n, value)
-        lhs = chunk_of(2, c)
-        for n in range(width // tile):
-            cols = pl.ds(n * tile, tile)
-            back[1, :, cols] += nt(lhs, wd_b[c, cols, :])
-
-        @pl.when(c + 1 < chunks)
-        def _():
-            down_x(c + 1).wait_recv()
-            down_m(c + 1, part).start()
-
-        for n in range(dc // rc):
-            behind(c * (dc // rc) + n)
-        return carry
 
     def own_back(c, carry):
         next_chunk(load_down, c)
         lhs = chunk_of(2, c)
         for n in range(width // tile):
             cols = pl.ds(n * tile, tile)
-            back[0, :, cols] += nt(lhs, bd[c % 2, cols, :])
+            back[0, :, cols] += nt(lhs, bd[c % depth_of, cols, :])
         return carry
 
-    first = min(4, chunks - 1)
-    lax.fori_loop(0, first, forward, 0)
-    load_down(first).wait()
-    load_down(0).start()
-    lax.fori_loop(0, chunks, own_back, 0)
-    invert(0)
-    load_down(first).start()
-    lax.fori_loop(first, chunks, forward, 0)
+    def partner_back(c, carry):
+        lhs = chunk_of(2, c)
+        for n in range(width // tile):
+            cols = pl.ds(n * tile, tile)
+            back[1, :, cols] += nt(lhs, wd_b[c, cols, :])
+        return carry
+
+    for k in range(2):
+        for i in range(3):
+            serve(k, i)
+    serve(2, 0)
+    serve(2, 1)
+    own_g.wait()
+    arrived(0)
+    arrived(1)
+    take_up(0)
+    take_up(1)
+    project(0, False, back.at[0])
+    activate(0, back.at[0])
+    serve(3, 0)
+    serve(3, 1)
+    serve(2, 2)
+    for i in range(2, n_up):
+        take_up(i)
+    for i in range(n_up):
+        up_m(i, 1 - part).wait_recv()
+    project(0, True, back.at[1])
+    activate(1, back.at[1])
+    hold = min(4, chunks - 2)
+    prime(load_down, 0, hold + 1)
+    clear(back.at[0])
+    clear(back.at[1])
+
+    def take_down(c):
+        down_x(c).wait_recv()
+        down_m(c, part).start()
+
+    take_down(0)
+    def forward(c, carry):
+        load_down(c).wait()
+        ahead = c + depth_of - 1
+
+        @pl.when(jnp.logical_and(ahead < chunks, jnp.logical_or(ahead <= hold, c > hold)))
+        def _():
+            load_down(ahead).start()
+
+        down_m(c, 1 - part).wait_recv()
+        for n in range(dc // rc):
+            cols = pl.ds(n * rc, rc)
+            value = nn(act[0], bd[c % depth_of, :, cols]) + nn(act[1], wd_b[c, :, cols])
+            store(c * (dc // rc) + n, value)
+
+        @pl.when(c + 2 < chunks)
+        def _():
+            take_down(c + 1)
+
+        @pl.when(c == 0)
+        def _():
+            serve(3, 2)
+
+        @pl.when(c == hold - 2)
+        def _():
+            arrived(2)
+            project(1, False, pre.at[0])
+            prepare_b(0)
+
+        @pl.when(c == hold - 1)
+        def _():
+            project(1, True, pre.at[1])
+            prepare_b(1)
+
+        @pl.when(c == hold)
+        def _():
+            arrived(3)
+            prime(load_down, 0, chunks)
+            lax.fori_loop(0, chunks, own_back, 0)
+            prime(load_down, hold + 1, chunks)
+            prime(load_fine, 0, fine)
+            lax.fori_loop(0, hold + 1, partner_back, 0)
+
+        @pl.when(c > hold)
+        def _():
+            partner_back(c, 0)
+
+        for n in range(dc // rc):
+            behind(c * (dc // rc) + n)
+
+        @pl.when(c == hold + 1)
+        def _():
+            invert(0)
+
+        @pl.when(c + 2 == chunks)
+        def _():
+            take_down(c + 1)
+
+        return carry
+
+    lax.fori_loop(0, chunks, forward, 0)
     invert(1)
 
     def score_copy(i, slot):
@@ -910,7 +990,7 @@
     def backward(c, carry):
         next_chunk(load_fine, c, fine)
         q = fine + c
-        value = nt(inner[0], bu[c % 2, :rc, :]) + nt(inner[1], wu_b[fine_columns(c), :])
+        value = nt(inner[0], bu[c % depth_of, :rc, :]) + nt(inner[1], wu_b[fine_columns(c), :])
         store(q, value)
         behind(q)
 
@@ -980,25 +1060,32 @@
     slope = inv * inv * inv * (dots / depth)
     for c in range(chunks):
         cols = pl.ds(c * dc, dc)
-        grad = g[:, cols].astype(jnp.float32) + inv * lifted[:, cols]
-        grad = grad - hid_b[:, cols].astype(jnp.float32) * slope
-        out_b[:, cols] = grad.astype(out_b.dtype)
+        hidden = hid_b[:, cols].astype(jnp.float32)
+        out_b[:, cols] = inv * lifted[:, cols] - hidden * slope
     for i in range(3):
         grad_copy(i).wait_recv()
-    rg_out[...] = rg_buf[0:1, :] + rg_in[0, 0:1, :] + rg_in[1, 1:2, :] + rg_in[2, 1:2, :]
+    rg_out[0:1, :] = rg_buf[0:1, :] + rg_in[0, 0:1, :]
+    rg_out[1:2, :] = rg_in[1, 1:2, :] + rg_in[2, 1:2, :]
 
     for k in range(4):
         z_send(k, pair).wait_send()
         z_send(k, opposite).wait_send()
 
-        @pl.when(middle)
-        def _():
+        if k == 0:
             z_send(k, other).wait_send()
-            z_relay(k).wait_send()
-
-        cross(k, z).wait_send()
+        else:
+
+            @pl.when(middle)
+            def _():
+                z_send(k, other).wait_send()
+                z_relay(k).wait_send()
+
         y_send(k).wait_send()
-        y_half(k, y).wait_send()
+        if k < 2:
+            y_copy(k, pair, y).wait_send()
+        else:
+            cross(k, z).wait_send()
+            y_half(k, y).wait_send()
         for source in (opposite, other):
             y_copy(k, source, y).wait_send()
     for i in range(n_up):
@@ -1026,6 +1113,7 @@
 
 N_UP = 4
 RING = 8
+AHEAD = 3
 
 
 def fused_plan(n, tok, depth, width):
@@ -1042,8 +1130,8 @@
         ((slots, tok, 128), f32),
         ((depth, width), bf),
         ((chunks, width, dc), bf),
-        ((2, dc, width), bf),
-        ((2, width, dc), bf),
+        ((AHEAD, dc, width), bf),
+        ((AHEAD, width, dc), bf),
         ((2, m_rows, width), bf),
         ((2, m_rows, width), f32),
         ((2, m_rows, width), f32),
@@ -1068,13 +1156,13 @@
         + [(4, planes + 1)] * 2
         + [(4, planes)] * 2
         + [(N_UP + chunks,)] * 4
-        + [(2,)] * 2
+        + [(AHEAD,)] * 2
         + [(steps,)] * 5
         + [(slots - 1,)] * 2
         + [(3,)] * 2
     )
     total = sum(math.prod(shape) * jnp.dtype(kind).itemsize for shape, kind in buffers)
-    fits = total + 5 * tok * depth * 2 < 64_500_000 and 3 * n <= 128 and planes == 4
+    fits = total + 7 * tok * depth * 2 < 64_500_000 and 3 * n <= 128 and planes == 4
     return fits, (planes, tok, depth, width, dc, rc, N_UP, RING), buffers, sems
 
 
@@ -1086,9 +1174,9 @@
     return pl.pallas_call(
         functools.partial(fused_kernel, dims + (lax.axis_size("pipe"),)),
         out_shape=[
-            jax.ShapeDtypeStruct((tok, depth), jnp.bfloat16),
-            jax.ShapeDtypeStruct((tok, depth), jnp.bfloat16),
-            jax.ShapeDtypeStruct((1, depth), jnp.float32),
+            jax.ShapeDtypeStruct((tok, depth), jnp.float32),
+            jax.ShapeDtypeStruct((tok, depth), jnp.float32),
+            jax.ShapeDtypeStruct((2, depth), jnp.float32),
         ],
         in_specs=[vmem] * 6 + [hbm] * 2,
         out_specs=[vmem] * 3,
@@ -1103,18 +1191,20 @@
 def on_device_fused(
     plan, hidden_a, routes_a, hidden_b, routes_b, grad_out_b, router, w_up, w_down
 ):
-    outs = fused(
+    mixed, delta, terms = fused(
         plan,
         hidden_a[0],
         hidden_b[0],
         grad_out_b[0],
-        routes_a[0],
-        routes_b[0],
+        routes_a[0].T,
+        routes_b[0].T,
         router[0],
         w_up[0, 0],
         w_down[0, 0],
     )
-    return tuple(o[None] for o in outs)
+    layer_out = (hidden_a[0].astype(jnp.float32) + mixed).astype(jnp.bfloat16)
+    grad_in = (grad_out_b[0].astype(jnp.float32) + delta).astype(jnp.bfloat16)
+    return (layer_out[None], grad_in[None], jnp.sum(terms, axis=0)[None, None])
 
 
 def solution(mesh):

time: 253 us -> 238 us (0.941)
  Pallas kernels: 244 us -> 233 us
  local copies, waits for them, and re-layouts: 7.71 us -> 0.61 us
  other arithmetic: 0 us -> 3.57 us
    pallas_call x1, Pallas kernels: 244 us -> 233 us  [fused(): pl.pallas_call(functools.partial(fused_kernel, dims + (lax.axis_size('pip...]
    unnamed x5 -> x0, local copies, waits for them, and re-layouts: 7.71 us -> none
    broadcast_in_dim x0 -> x1, other arithmetic: none -> 2.78 us  [on_device_fused(): return (layer_out[None], grad_in[None], jnp.sum(terms, axis=0)[None, None])]
where the time goes in v3:
time: 238 us
  Pallas kernels  233 us (98%)
  other arithmetic  3.57 us (2%)
    pallas_call x1, Pallas kernels, fused(): pl.pallas_call(functools.partial(fused_kernel, dims + (lax.axis_size('pip...  233 us

profile of v3, /device:TPU:0, one launch (start us, length us, event | category | flops | bytes accessed | tf_op | source)
XLA Modules:
  0.0 238.1 jit_solution(10322178651853661364)
XLA Ops:
  0.6 233.3 %shard_map.103 = (f32[64,3584]{1,0:T(8,128)}, f32[64,3584]{1,0:T(8,128)}, f32[2,3584]{1,0:T(2,128)}) custom-call(bf16[64,3584]{1,0:T(8,128)(2,1)} %bitcast.20, bf16[64,3584]{1,0:T(8,128)(2,1)} %bitcast.22, bf16[64,3584]{1,0:T(8,128)(2,1)} %bitcast.21, s32[8,64]{1,0:T(8,128)} %bitcast.24, s32[8,64]{1,0:T(8,128)} %bitcast.25, bf16[16,3584]{1,0:T(8,128)(2,1)} %bitcast.23, ...), custom_call_target="tpu_custom_call" | custom-call | tf_op jit(solution)/shard_map/pallas_call | solution.py:1174
  234.0 2.8 %fusion = (bf16[1,64,3584]{2,1,0:T(8,128)(2,1)}, bf16[1,64,3584]{2,1,0:T(8,128)(2,1)}) fusion(f32[64,3584]{1,0:T(8,128)} %get-tuple-element.6, bf16[1,64,3584]{2,1,0:T(8,128)(2,1)} %param.8, f32[64,3584]{1,0:T(8,128)} %get-tuple-element.7, bf16[1,64,3584]{2,1,0:T(8,128)(2,1)} %param.12), kind=kLoop, calls=%fused_computation.2 | loop fusion | flops 1376256 | bytes 3670016 | tf_op jit(solution)/shard_map/broadcast_in_dim | solution.py:1207
  236.7 0.8 reduce_sum.9
  237.5 0.6 broadcast_in_dim.11

commit v4 on v3

--- a/solution.py
+++ b/solution.py
@@ -426,7 +426,7 @@
 
 
 def fused_kernel(dims, *refs):
-    planes, tok, depth, width, dc, rc, n_up, ring, n_pipe = dims
+    planes, tok, depth, width, kc, dc, rc, n_up, ring, n_pipe = dims
     (hid_a, hid_b, g, routes_a, routes_b, router, wu, wd, out_a, out_b, rg_out) = refs[:11]
     (rows, tabs, wu_b, wd_b, bu, bd, act, pre, back, silu, inner) = refs[11:22]
     (o_buf, y_buf, t_buf, z_buf, f_buf, sc_col, sc_own, sc_all, rg_buf, rg_in) = refs[22:32]
@@ -485,51 +485,6 @@
     own_g = pltpu.make_async_copy(g, rows.at[2, slot_me], own_s.at[0])
     own_g.start()
 
-    def nn(lhs, rhs):
-        return jnp.dot(lhs, rhs, preferred_element_type=jnp.float32)
-
-    def nt(lhs, rhs):
-        return lax.dot_general(
-            lhs, rhs, (((1,), (1,)), ((), ())), preferred_element_type=jnp.float32
-        )
-
-    def normalize(k, src):
-        step = 16
-
-        def body(i, carry):
-            r = pl.ds(pl.multiple_of(i * step, step), step)
-            h = src[r, :].astype(jnp.float32)
-            rinv = lax.rsqrt(jnp.mean(h * h, axis=-1, keepdims=True) + EPSILON)
-            rows[k, slot_me, r, :] = (h * rinv).astype(rows.dtype)
-            if k == 1:
-                rinv_b[r, :] = jnp.broadcast_to(rinv, (step, lanes))
-            return carry
-
-        lax.fori_loop(0, tok // step, body, 0)
-
-    normalize(0, hid_a)
-    normalize(1, hid_b)
-    for i in range(3):
-        router_t[i * experts : (i + 1) * experts] = router[...]
-    router_t[3 * experts :] = jnp.zeros((lanes - 3 * experts, depth), router_t.dtype)
-    lane = lax.broadcasted_iota(jnp.int32, (tok, lanes), 1)
-    expert_lane = lax.rem(lane, experts)
-
-    def affinity(k, routes, section):
-        logits = nt(rows[k, slot_me], router_t[...])
-        named = routes[...].T
-        chosen = expert_lane == named[:, 0:1]
-        for i in range(1, named.shape[1]):
-            chosen = jnp.logical_or(chosen, expert_lane == named[:, i : i + 1])
-        sig = jnp.where(chosen, jax.nn.sigmoid(logits), 0.0)
-        here = jnp.where(lax.div(lane, experts) == section, sig, 0.0)
-        return sig, here, jnp.sum(here, axis=-1, keepdims=True)
-
-    _, here_a, total_a = affinity(0, routes_a, 0)
-    sig_b, here_b, total_b = affinity(1, routes_b, 1)
-    slope_b = jnp.where(lax.div(lane, experts) == 2, sig_b * (1.0 - sig_b), 0.0)
-    tabs[slot_me] = here_a / total_a + here_b / total_b + slope_b / total_b
-
     pl.semaphore_wait(barrier, slots - 1 + 3)
 
     def up_region(which, i):
@@ -548,6 +503,9 @@
 
     def columns(c):
         return pl.ds(pl.multiple_of(c * dc, dc), dc)
+
+    def wide_columns(c):
+        return pl.ds(pl.multiple_of(c * kc, kc), kc)
 
     def fine_columns(c):
         return pl.ds(pl.multiple_of(c * rc, rc), rc)
@@ -608,7 +566,8 @@
         return copy(ref, ref, ys.at[k, pair], yr.at[k, pair], y_near)
 
     def spread(k):
-        y_send(k).start()
+        if k < 3:
+            y_send(k).start()
 
         @pl.when(middle)
         def _():
@@ -658,11 +617,58 @@
         y_copy(k, opposite, 1 - y).wait_recv()
         y_copy(k, other, 1 - y).wait_recv()
 
+    y_send(3).start()
+
+    def nn(lhs, rhs):
+        return jnp.dot(lhs, rhs, preferred_element_type=jnp.float32)
+
+    def nt(lhs, rhs):
+        return lax.dot_general(
+            lhs, rhs, (((1,), (1,)), ((), ())), preferred_element_type=jnp.float32
+        )
+
+    def normalize(k, src):
+        step = 16
+
+        def body(i, carry):
+            r = pl.ds(pl.multiple_of(i * step, step), step)
+            h = src[r, :].astype(jnp.float32)
+            rinv = lax.rsqrt(jnp.mean(h * h, axis=-1, keepdims=True) + EPSILON)
+            rows[k, slot_me, r, :] = (h * rinv).astype(rows.dtype)
+            if k == 1:
+                rinv_b[r, :] = jnp.broadcast_to(rinv, (step, lanes))
+            return carry
+
+        lax.fori_loop(0, tok // step, body, 0)
+
+    normalize(0, hid_a)
+    normalize(1, hid_b)
+    for i in range(3):
+        router_t[i * experts : (i + 1) * experts] = router[...]
+    router_t[3 * experts :] = jnp.zeros((lanes - 3 * experts, depth), router_t.dtype)
+    lane = lax.broadcasted_iota(jnp.int32, (tok, lanes), 1)
+    expert_lane = lax.rem(lane, experts)
+
+    def affinity(k, routes, section):
+        logits = nt(rows[k, slot_me], router_t[...])
+        named = routes[...].T
+        chosen = expert_lane == named[:, 0:1]
+        for i in range(1, named.shape[1]):
+            chosen = jnp.logical_or(chosen, expert_lane == named[:, i : i + 1])
+        sig = jnp.where(chosen, jax.nn.sigmoid(logits), 0.0)
+        here = jnp.where(lax.div(lane, experts) == section, sig, 0.0)
+        return sig, here, jnp.sum(here, axis=-1, keepdims=True)
+
+    _, here_a, total_a = affinity(0, routes_a, 0)
+    sig_b, here_b, total_b = affinity(1, routes_b, 1)
+    slope_b = jnp.where(lax.div(lane, experts) == 2, sig_b * (1.0 - sig_b), 0.0)
+    tabs[slot_me] = here_a / total_a + here_b / total_b + slope_b / total_b
+
     for k in range(4):
         spread(k)
 
-    def chunk_of(k, c):
-        return rows[k, :, :, columns(c)].reshape(m_rows, dc)
+    def chunk_of(k, cols):
+        return rows[k, :, :, cols].reshape(m_rows, cols.size)
 
     class Pieces:
         def __init__(self, src, dst, sem):
@@ -684,13 +690,14 @@
     depth_of = bu.shape[0]
 
     def load_up(c):
-        return Pieces(wu.at[columns(c)], bu.at[c % depth_of], bus.at[c % depth_of])
+        return Pieces(wu.at[wide_columns(c)], bu.at[c % depth_of], bus.at[c % depth_of])
 
     def load_fine(c):
         return Pieces(wu.at[fine_columns(c)], bu.at[c % depth_of, pl.ds(0, rc)], bus.at[c % depth_of])
 
     def load_down(c):
-        return Pieces(wd.at[:, columns(c)], bd.at[c % depth_of], bds.at[c % depth_of])
+        dst = bd.at[c % depth_of, :, pl.ds(0, dc)]
+        return Pieces(wd.at[:, columns(c)], dst, bds.at[c % depth_of])
 
     def prime(load, lo, hi):
         for c in range(lo, min(hi, lo + depth_of - 1)):
@@ -715,20 +722,21 @@
 
     def project(k, partner, dst):
         clear(dst)
+        count = depth // kc
         if not partner:
-            prime(load_up, 0, chunks)
+            prime(load_up, 0, count)
 
         def body(c, carry):
             if not partner:
-                next_chunk(load_up, c)
-            lhs = chunk_of(k, c)
+                next_chunk(load_up, c, count)
+            lhs = chunk_of(k, wide_columns(c))
             for n in range(width // tile):
                 cols = pl.ds(n * tile, tile)
-                rhs = wu_b[columns(c), cols] if partner else bu[c % depth_of, :, cols]
+                rhs = wu_b[wide_columns(c), cols] if partner else bu[c % depth_of, :, cols]
                 dst[:, cols] += nn(lhs, rhs)
             return carry
 
-        lax.fori_loop(0, chunks, body, 0)
+        lax.fori_loop(0, count, body, 0)
 
     def pick(s, column):
         return jnp.sum(jnp.where(lane == column, tabs[s], 0.0), axis=-1, keepdims=True)
@@ -875,16 +883,19 @@
         up_x(i).wait_recv()
         up_m(i, part).start()
 
+    def load_wide(c):
+        return Pieces(wd.at[:, wide_columns(c)], bd.at[c % depth_of], bds.at[c % depth_of])
+
     def own_back(c, carry):
-        next_chunk(load_down, c)
-        lhs = chunk_of(2, c)
+        next_chunk(load_wide, c, depth // kc)
+        lhs = chunk_of(2, wide_columns(c))
         for n in range(width // tile):
             cols = pl.ds(n * tile, tile)
             back[0, :, cols] += nt(lhs, bd[c % depth_of, cols, :])
         return carry
 
     def partner_back(c, carry):
-        lhs = chunk_of(2, c)
+        lhs = chunk_of(2, columns(c))
         for n in range(width // tile):
             cols = pl.ds(n * tile, tile)
             back[1, :, cols] += nt(lhs, wd_b[c, cols, :])
@@ -902,16 +913,22 @@
     take_up(1)
     project(0, False, back.at[0])
     activate(0, back.at[0])
-    serve(3, 0)
-    serve(3, 1)
     serve(2, 2)
+
+    def serve_last():
+        serve(3, 0)
+        serve(3, 1)
+
+    pl.when(middle)(serve_last)
     for i in range(2, n_up):
         take_up(i)
     for i in range(n_up):
         up_m(i, 1 - part).wait_recv()
     project(0, True, back.at[1])
     activate(1, back.at[1])
-    hold = min(4, chunks - 2)
+    pl.when(jnp.logical_not(middle))(serve_last)
+    marks = [chunks * i // 14 for i in (3, 5, 7, 9)]
+    hold = marks[2]
     prime(load_down, 0, hold + 1)
     clear(back.at[0])
     clear(back.at[1])
@@ -921,6 +938,7 @@
         down_m(c, part).start()
 
     take_down(0)
+    take_down(1)
     def forward(c, carry):
         load_down(c).wait()
         ahead = c + depth_of - 1
@@ -935,21 +953,17 @@
             value = nn(act[0], bd[c % depth_of, :, cols]) + nn(act[1], wd_b[c, :, cols])
             store(c * (dc // rc) + n, value)
 
-        @pl.when(c + 2 < chunks)
-        def _():
-            take_down(c + 1)
-
         @pl.when(c == 0)
         def _():
             serve(3, 2)
 
-        @pl.when(c == hold - 2)
+        @pl.when(c == marks[0])
         def _():
             arrived(2)
             project(1, False, pre.at[0])
             prepare_b(0)
 
-        @pl.when(c == hold - 1)
+        @pl.when(c == marks[1])
         def _():
             project(1, True, pre.at[1])
             prepare_b(1)
@@ -957,22 +971,28 @@
         @pl.when(c == hold)
         def _():
             arrived(3)
-            prime(load_down, 0, chunks)
-            lax.fori_loop(0, chunks, own_back, 0)
+            prime(load_wide, 0, depth // kc)
+            lax.fori_loop(0, depth // kc, own_back, 0)
             prime(load_down, hold + 1, chunks)
             prime(load_fine, 0, fine)
-            lax.fori_loop(0, hold + 1, partner_back, 0)
-
-        @pl.when(c > hold)
+
+        @pl.when(c == marks[3])
+        def _():
+            lax.fori_loop(0, marks[3] + 1, partner_back, 0)
+            invert(0)
+
+        @pl.when(c > marks[3])
         def _():
             partner_back(c, 0)
 
-        for n in range(dc // rc):
-            behind(c * (dc // rc) + n)
-
-        @pl.when(c == hold + 1)
-        def _():
-            invert(0)
+        @pl.when(c + 1 < chunks)
+        def _():
+            for n in range(dc // rc):
+                behind(c * (dc // rc) + n)
+
+        @pl.when(c + 3 < chunks)
+        def _():
+            take_down(c + 2)
 
         @pl.when(c + 2 == chunks)
         def _():
@@ -992,7 +1012,7 @@
         q = fine + c
         value = nt(inner[0], bu[c % depth_of, :rc, :]) + nt(inner[1], wu_b[fine_columns(c), :])
         store(q, value)
-        behind(q)
+        behind(q - 1)
 
         @pl.when(c == 1)
         def _():
@@ -1028,9 +1048,9 @@
         return (high, medium, (rest - medium.astype(jnp.float32)).astype(jnp.bfloat16))
 
     pieces = thirds(both)
-    for c in range(chunks):
-        cols = pl.ds(c * dc, dc)
-        rhs = rows[1, :, :, cols].reshape(m_rows, dc)
+    for c in range(depth // kc):
+        cols = pl.ds(c * kc, kc)
+        rhs = rows[1, :, :, cols].reshape(m_rows, kc)
         rg_buf[:, cols] = nn(pieces[0], rhs) + nn(pieces[1], rhs) + nn(pieces[2], rhs)
 
     def grad_copy(i):
@@ -1042,7 +1062,7 @@
         grad_copy(i).start()
     padded = jnp.concatenate([logit, jnp.zeros((lanes - experts, m_rows), jnp.float32)], axis=0)
     sc_col[...] = padded.T.reshape(slots, tok, lanes)
-    for q in range(steps, steps + 3):
+    for q in range(steps - 1, steps + 3):
         behind(q)
     dense = thirds(sc_col[slot_me])
     for q in range(steps + 3, steps + lags[-1][0]):
@@ -1050,16 +1070,16 @@
 
     inv = rinv_b[:, 0:1]
     dots = jnp.zeros((tok, 1), jnp.float32)
-    for c in range(chunks):
-        cols = pl.ds(c * dc, dc)
+    for c in range(depth // kc):
+        cols = pl.ds(c * kc, kc)
         rhs = router_t[:, cols]
         extra = nn(dense[0], rhs) + nn(dense[1], rhs) + nn(dense[2], rhs)
         v = ROUTED_SCALE * lifted[:, cols] + extra
         lifted[:, cols] = v
         dots = dots + jnp.sum(v * hid_b[:, cols].astype(jnp.float32), axis=-1, keepdims=True)
     slope = inv * inv * inv * (dots / depth)
-    for c in range(chunks):
-        cols = pl.ds(c * dc, dc)
+    for c in range(depth // kc):
+        cols = pl.ds(c * kc, kc)
         hidden = hid_b[:, cols].astype(jnp.float32)
         out_b[:, cols] = inv * lifted[:, cols] - hidden * slope
     for i in range(3):
@@ -1120,8 +1140,8 @@
     planes = n // PLANE
     slots = 2 * planes
     m_rows = slots * tok
-    dc = 512 if depth % 512 == 0 else 256
-    rc = 256
+    kc = 512 if depth % 512 == 0 else 256
+    dc = rc = 256
     chunks = depth // dc
     steps = 2 * (depth // rc)
     bf, f32 = jnp.bfloat16, jnp.float32
@@ -1130,8 +1150,8 @@
         ((slots, tok, 128), f32),
         ((depth, width), bf),
         ((chunks, width, dc), bf),
-        ((AHEAD, dc, width), bf),
-        ((AHEAD, width, dc), bf),
+        ((AHEAD, kc, width), bf),
+        ((AHEAD, width, kc), bf),
         ((2, m_rows, width), bf),
         ((2, m_rows, width), f32),
         ((2, m_rows, width), f32),
@@ -1163,7 +1183,7 @@
     )
     total = sum(math.prod(shape) * jnp.dtype(kind).itemsize for shape, kind in buffers)
     fits = total + 7 * tok * depth * 2 < 64_500_000 and 3 * n <= 128 and planes == 4
-    return fits, (planes, tok, depth, width, dc, rc, N_UP, RING), buffers, sems
+    return fits, (planes, tok, depth, width, kc, dc, rc, N_UP, RING), buffers, sems
 
 
 def fused(plan, *args):

time: 238 us -> 230 us (0.966)
  Pallas kernels: 233 us -> 225 us
    pallas_call x1, Pallas kernels: 233 us -> 225 us  [fused(): pl.pallas_call(functools.partial(fused_kernel, dims + (lax.axis_size('pip...]
where the time goes in v4:
time: 230 us
  Pallas kernels  225 us (98%)
  other arithmetic  3.57 us (2%)
    pallas_call x1, Pallas kernels, fused(): pl.pallas_call(functools.partial(fused_kernel, dims + (lax.axis_size('pip...  225 us

profile of v4, /device:TPU:0, one launch (start us, length us, event | category | flops | bytes accessed | tf_op | source)
XLA Modules:
  0.0 229.7 jit_solution(14747456590724569464)
XLA Ops:
  0.6 224.9 %shard_map.103 = (f32[64,3584]{1,0:T(8,128)}, f32[64,3584]{1,0:T(8,128)}, f32[2,3584]{1,0:T(2,128)}) custom-call(bf16[64,3584]{1,0:T(8,128)(2,1)} %bitcast.20, bf16[64,3584]{1,0:T(8,128)(2,1)} %bitcast.22, bf16[64,3584]{1,0:T(8,128)(2,1)} %bitcast.21, s32[8,64]{1,0:T(8,128)} %bitcast.24, s32[8,64]{1,0:T(8,128)} %bitcast.25, bf16[16,3584]{1,0:T(8,128)(2,1)} %bitcast.23, ...), custom_call_target="tpu_custom_call" | custom-call | tf_op jit(solution)/shard_map/pallas_call | solution.py:1194
  225.5 2.8 %fusion = (bf16[1,64,3584]{2,1,0:T(8,128)(2,1)}, bf16[1,64,3584]{2,1,0:T(8,128)(2,1)}) fusion(f32[64,3584]{1,0:T(8,128)} %get-tuple-element.6, bf16[1,64,3584]{2,1,0:T(8,128)(2,1)} %param.8, f32[64,3584]{1,0:T(8,128)} %get-tuple-element.7, bf16[1,64,3584]{2,1,0:T(8,128)(2,1)} %param.12), kind=kLoop, calls=%fused_computation.2 | loop fusion | flops 1376256 | bytes 3670016 | tf_op jit(solution)/shard_map/broadcast_in_dim | solution.py:1227
  228.3 0.8 reduce_sum.9
  229.1 0.6 broadcast_in_dim.11

commit v5 on v4

--- a/solution.py
+++ b/solution.py
@@ -430,9 +430,9 @@
     (hid_a, hid_b, g, routes_a, routes_b, router, wu, wd, out_a, out_b, rg_out) = refs[:11]
     (rows, tabs, wu_b, wd_b, bu, bd, act, pre, back, silu, inner) = refs[11:22]
     (o_buf, y_buf, t_buf, z_buf, f_buf, sc_col, sc_own, sc_all, rg_buf, rg_in) = refs[22:32]
-    (router_t, rinv_b, lifted) = refs[32:35]
-    (own_s, zs, zr, ys, yr, xs, xr, ms, mr, bus, bds) = refs[35:46]
-    (rys, ryr, rzs, rzr, rfs, scs, scr, gs, gr) = refs[46:55]
+    (router_t, rinv_b, mixed, extra, dots, lifted) = refs[32:38]
+    (own_s, zs, zr, ys, yr, xs, xr, ms, mr, bus, bds) = refs[38:49]
+    (rys, ryr, rzs, rzr, rfs, scs, scr, gs, gr) = refs[49:58]
     slots = 2 * planes
     experts = 2 * slots
     m_rows = slots * tok
@@ -792,6 +792,9 @@
         src = t_buf.at[q % ring, other]
         return copy(src, f_buf.at[q], rzs.at[q], rfs.at[q], chip(pair, y))
 
+    def direct(q):
+        return isinstance(q, int) and q >= steps - 1
+
     def sent_z(q):
         src = t_buf.at[q % ring, pl.ds(0, planes - 1)]
         dst = z_buf.at[q, pl.ds(0, planes - 1)]
@@ -811,7 +814,12 @@
         for k in range(planes):
             first = o_buf[q % ring, y * planes + k].astype(jnp.float32)
             t_buf[q % ring, k] = (first + y_buf[q, k].astype(jnp.float32)).astype(t_buf.dtype)
-        rs_z(q, pair, 0).start()
+        if direct(q):
+            pl.when(middle)(lambda: rs_z(q, opposite, 1).start())
+            rs_z(q, other, 2).start()
+            pl.when(jnp.logical_not(middle))(lambda: rs_z(q, opposite, 1).start())
+            rs_z(q, pair, 0).start()
+            return
 
         @pl.when(middle)
         def _():
@@ -822,7 +830,12 @@
             rs_far(q).start()
             rs_z(q, opposite, 1).start()
 
+        rs_z(q, pair, 0).start()
+
     def relay_z(q):
+        if direct(q):
+            return
+
         @pl.when(middle)
         def _():
             rs_far(q).wait_recv()
@@ -839,19 +852,31 @@
             total = total + z_buf[q, i].astype(jnp.float32)
         return total
 
+    def finish_b(c, total):
+        cols = fine_columns(c)
+        v = ROUTED_SCALE * total + extra[:, cols]
+        lifted[:, cols] = v
+        prod = v * hid_b[:, cols].astype(jnp.float32)
+        for i in range(rc // lanes):
+            dots[...] += prod[:, i * lanes : (i + 1) * lanes]
+
     def fold_z(q):
         def settle(total):
             def of_a():
-                out_a[:, fine_columns(q)] = ROUTED_SCALE * total
+                mixed[:, fine_columns(q)] = (ROUTED_SCALE * total).astype(mixed.dtype)
 
             def of_b():
                 lifted[:, fine_columns(q - fine)] = total
 
             if isinstance(q, int):
-                of_a() if q < fine else of_b()
+                finish_b(q - fine, total)
             else:
                 pl.when(q < fine)(of_a)
                 pl.when(q >= fine)(of_b)
+
+        if direct(q):
+            settle(take_z(q, planes - 1))
+            return
 
         @pl.when(middle)
         def _():
@@ -1007,12 +1032,18 @@
         target = of_slot((slot_me + i) % slots)
         return copy(sc_own, sc_all.at[slot], scs.at[i - 1], scr.at[i - 1], target)
 
+    save_a = pltpu.make_async_copy(mixed, out_a, own_s.at[1])
+
     def backward(c, carry):
         next_chunk(load_fine, c, fine)
         q = fine + c
         value = nt(inner[0], bu[c % depth_of, :rc, :]) + nt(inner[1], wu_b[fine_columns(c), :])
         store(q, value)
         behind(q - 1)
+
+        @pl.when(c == min(lags[-1][0] + 1, fine - 1))
+        def _():
+            save_a.start()
 
         @pl.when(c == 1)
         def _():
@@ -1062,31 +1093,35 @@
         grad_copy(i).start()
     padded = jnp.concatenate([logit, jnp.zeros((lanes - experts, m_rows), jnp.float32)], axis=0)
     sc_col[...] = padded.T.reshape(slots, tok, lanes)
-    for q in range(steps - 1, steps + 3):
-        behind(q)
     dense = thirds(sc_col[slot_me])
-    for q in range(steps + 3, steps + lags[-1][0]):
-        behind(q)
-
-    inv = rinv_b[:, 0:1]
-    dots = jnp.zeros((tok, 1), jnp.float32)
+    dots[...] = jnp.zeros(dots.shape, jnp.float32)
     for c in range(depth // kc):
         cols = pl.ds(c * kc, kc)
         rhs = router_t[:, cols]
-        extra = nn(dense[0], rhs) + nn(dense[1], rhs) + nn(dense[2], rhs)
-        v = ROUTED_SCALE * lifted[:, cols] + extra
-        lifted[:, cols] = v
-        dots = dots + jnp.sum(v * hid_b[:, cols].astype(jnp.float32), axis=-1, keepdims=True)
-    slope = inv * inv * inv * (dots / depth)
+        extra[:, cols] = nn(dense[0], rhs) + nn(dense[1], rhs) + nn(dense[2], rhs)
+    for q in range(fine, steps - 1 - lags[-1][0]):
+        finish_b(q - fine, lifted[:, fine_columns(q - fine)])
+    relay_z(steps - 7)
+    for q in range(steps - 5, steps):
+        fold_y(q)
+        relay_z(q - 1)
+        fold_z(q - 4)
+    relay_z(steps - 1)
+    for q in range(steps - 4, steps):
+        fold_z(q)
+
+    inv = rinv_b[:, 0:1]
+    slope = inv * inv * inv * (jnp.sum(dots[...], axis=-1, keepdims=True) / depth)
     for c in range(depth // kc):
         cols = pl.ds(c * kc, kc)
-        hidden = hid_b[:, cols].astype(jnp.float32)
-        out_b[:, cols] = inv * lifted[:, cols] - hidden * slope
+        delta = inv * lifted[:, cols] - hid_b[:, cols].astype(jnp.float32) * slope
+        out_b[:, cols] = delta.astype(out_b.dtype)
     for i in range(3):
         grad_copy(i).wait_recv()
     rg_out[0:1, :] = rg_buf[0:1, :] + rg_in[0, 0:1, :]
     rg_out[1:2, :] = rg_in[1, 1:2, :] + rg_in[2, 1:2, :]
 
+    save_a.wait()
     for k in range(4):
         z_send(k, pair).wait_send()
         z_send(k, opposite).wait_send()
@@ -1169,10 +1204,13 @@
         ((3, 8, depth), f32),
         ((128, depth), bf),
         ((tok, 128), f32),
+        ((tok, depth), bf),
+        ((tok, depth), f32),
+        ((tok, 128), f32),
         ((tok, depth), f32),
     ]
     sems = (
-        [(1,)]
+        [(2,)]
         + [(4, planes + 1)] * 2
         + [(4, planes)] * 2
         + [(N_UP + chunks,)] * 4
@@ -1182,7 +1220,7 @@
         + [(3,)] * 2
     )
     total = sum(math.prod(shape) * jnp.dtype(kind).itemsize for shape, kind in buffers)
-    fits = total + 7 * tok * depth * 2 < 64_500_000 and 3 * n <= 128 and planes == 4
+    fits = total + 4 * tok * depth * 2 < 64_500_000 and 3 * n <= 128 and planes == 4
     return fits, (planes, tok, depth, width, kc, dc, rc, N_UP, RING), buffers, sems
 
 
@@ -1194,12 +1232,12 @@
     return pl.pallas_call(
         functools.partial(fused_kernel, dims + (lax.axis_size("pipe"),)),
         out_shape=[
-            jax.ShapeDtypeStruct((tok, depth), jnp.float32),
-            jax.ShapeDtypeStruct((tok, depth), jnp.float32),
+            jax.ShapeDtypeStruct((tok, depth), jnp.bfloat16),
+            jax.ShapeDtypeStruct((tok, depth), jnp.bfloat16),
             jax.ShapeDtypeStruct((2, depth), jnp.float32),
         ],
         in_specs=[vmem] * 6 + [hbm] * 2,
-        out_specs=[vmem] * 3,
+        out_specs=[hbm, vmem, vmem],
         scratch_shapes=[pltpu.VMEM(shape, kind) for shape, kind in buffers]
         + [DMA(shape) for shape in sems],
         compiler_params=pltpu.CompilerParams(
@@ -1222,8 +1260,8 @@
         w_up[0, 0],
         w_down[0, 0],
     )
-    layer_out = (hidden_a[0].astype(jnp.float32) + mixed).astype(jnp.bfloat16)
-    grad_in = (grad_out_b[0].astype(jnp.float32) + delta).astype(jnp.bfloat16)
+    layer_out = (hidden_a[0].astype(jnp.float32) + mixed.astype(jnp.float32)).astype(jnp.bfloat16)
+    grad_in = (grad_out_b[0].astype(jnp.float32) + delta.astype(jnp.float32)).astype(jnp.bfloat16)
     return (layer_out[None], grad_in[None], jnp.sum(terms, axis=0)[None, None])
 
 

time: 230 us -> 227 us (0.987)
  Pallas kernels: 225 us -> 222 us
    pallas_call x1, Pallas kernels: 225 us -> 222 us  [fused(): pl.pallas_call(functools.partial(fused_kernel, dims + (lax.axis_size('pip...]
where the time goes in v5:
time: 227 us
  Pallas kernels  222 us (98%)
  other arithmetic  3.35 us (1%)
    pallas_call x1, Pallas kernels, fused(): pl.pallas_call(functools.partial(fused_kernel, dims + (lax.axis_size('pip...  222 us

profile of v5, /device:TPU:0, one launch (start us, length us, event | category | flops | bytes accessed | tf_op | source)
XLA Modules:
  0.0 227.0 jit_solution(3859329840577522359)
XLA Ops:
  0.6 222.4 %shard_map.103 = (bf16[64,3584]{1,0:T(8,128)(2,1)}, bf16[64,3584]{1,0:T(8,128)(2,1)}, f32[2,3584]{1,0:T(2,128)}) custom-call(bf16[64,3584]{1,0:T(8,128)(2,1)} %bitcast.20, bf16[64,3584]{1,0:T(8,128)(2,1)} %bitcast.22, bf16[64,3584]{1,0:T(8,128)(2,1)} %bitcast.21, s32[8,64]{1,0:T(8,128)} %bitcast.24, s32[8,64]{1,0:T(8,128)} %bitcast.25, ...), custom_call_target="tpu_custom_call" | custom-call | tf_op jit(solution)/shard_map/pallas_call | solution.py:1232
  223.1 2.6 %fusion = (bf16[1,64,3584]{2,1,0:T(8,128)(2,1)}, bf16[1,64,3584]{2,1,0:T(8,128)(2,1)}) fusion(bf16[64,3584]{1,0:T(8,128)(2,1)} %get-tuple-element.6, bf16[1,64,3584]{2,1,0:T(8,128)(2,1)} %param.8, bf16[64,3584]{1,0:T(8,128)(2,1)} %get-tuple-element.7, bf16[1,64,3584]{2,1,0:T(8,128)(2,1)} %param.12), kind=kLoop, calls=%fused_computation.2 | loop fusion | flops 1835008 | bytes 2752512 | tf_op jit(solution)/shard_map/broadcast_in_dim | solution.py:1265
  225.6 0.8 reduce_sum.9
  226.4 0.6 broadcast_in_dim.11

commit v6 on v5

--- a/solution.py
+++ b/solution.py
@@ -432,7 +432,7 @@
     (o_buf, y_buf, t_buf, z_buf, f_buf, sc_col, sc_own, sc_all, rg_buf, rg_in) = refs[22:32]
     (router_t, rinv_b, mixed, extra, dots, lifted) = refs[32:38]
     (own_s, zs, zr, ys, yr, xs, xr, ms, mr, bus, bds) = refs[38:49]
-    (rys, ryr, rzs, rzr, rfs, scs, scr, gs, gr) = refs[49:58]
+    (rys, ryr, rzs, rzr, rfs, scs, scr, gs, gr, lys, lyr) = refs[49:60]
     slots = 2 * planes
     experts = 2 * slots
     m_rows = slots * tok
@@ -784,6 +784,22 @@
         src = o_buf.at[q % ring, pl.ds((1 - y) * planes, planes)]
         return copy(src, y_buf.at[q], rys.at[q], ryr.at[q], y_near)
 
+    def rs_last(i):
+        q, plane = steps - 1, (other, opposite, pair, z)[i]
+        src = o_buf.at[q % ring, (1 - y) * planes + plane]
+        return copy(src, y_buf.at[q, plane], lys.at[i], lyr.at[i], y_near)
+
+    def fold_last():
+        q = steps - 1
+        sent_z(q - ring)
+        for i, plane in enumerate((other, opposite, pair, z)):
+            rs_last(i).wait_recv()
+            first = o_buf[q % ring, y * planes + plane].astype(jnp.float32)
+            both = first + y_buf[q, plane].astype(jnp.float32)
+            t_buf[q % ring, plane] = both.astype(t_buf.dtype)
+            if i < planes - 1:
+                rs_z(q, plane, (2, 1, 0)[i]).start()
+
     def rs_z(q, target, place_at):
         src = t_buf.at[q % ring, target]
         return copy(src, z_buf.at[q, place_at], rzs.at[q], rzr.at[q], chip(target, y))
@@ -902,7 +918,16 @@
 
         pl.when(q >= ring)(clean)
         o_buf[q % ring] = value.reshape(slots, tok, rc).astype(o_buf.dtype)
-        rs_y(q).start()
+
+        @pl.when(q < steps - 1)
+        def _():
+            rs_y(q).start()
+
+        @pl.when(q == steps - 1)
+        def _():
+            for i in range(planes):
+                rs_last(i).start()
+
 
     def take_up(i):
         up_x(i).wait_recv()
@@ -952,7 +977,7 @@
     project(0, True, back.at[1])
     activate(1, back.at[1])
     pl.when(jnp.logical_not(middle))(serve_last)
-    marks = [chunks * i // 14 for i in (3, 5, 7, 9)]
+    marks = [chunks * i // 14 for i in (0, 3, 6, 8)]
     hold = marks[2]
     prime(load_down, 0, hold + 1)
     clear(back.at[0])
@@ -978,15 +1003,15 @@
             value = nn(act[0], bd[c % depth_of, :, cols]) + nn(act[1], wd_b[c, :, cols])
             store(c * (dc // rc) + n, value)
 
-        @pl.when(c == 0)
-        def _():
-            serve(3, 2)
-
         @pl.when(c == marks[0])
         def _():
             arrived(2)
             project(1, False, pre.at[0])
             prepare_b(0)
+
+        @pl.when(c == 1)
+        def _():
+            serve(3, 2)
 
         @pl.when(c == marks[1])
         def _():
@@ -1103,7 +1128,7 @@
         finish_b(q - fine, lifted[:, fine_columns(q - fine)])
     relay_z(steps - 7)
     for q in range(steps - 5, steps):
-        fold_y(q)
+        fold_last() if q == steps - 1 else fold_y(q)
         relay_z(q - 1)
         fold_z(q - 4)
     relay_z(steps - 1)
@@ -1155,11 +1180,16 @@
     lax.fori_loop(0, chunks, drain, 0)
 
     def drain_rs(q, carry):
-        rs_y(q).wait_send()
+        @pl.when(q < steps - 1)
+        def _():
+            rs_y(q).wait_send()
+
         sent_z(q)
         return carry
 
     lax.fori_loop(steps - ring, steps, drain_rs, 0)
+    for i in range(planes):
+        rs_last(i).wait_send()
     for i in range(1, slots):
         score_copy(i, slot_me).wait_send()
     for i in range(3):
@@ -1218,6 +1248,7 @@
         + [(steps,)] * 5
         + [(slots - 1,)] * 2
         + [(3,)] * 2
+        + [(planes,)] * 2
     )
     total = sum(math.prod(shape) * jnp.dtype(kind).itemsize for shape, kind in buffers)
     fits = total + 4 * tok * depth * 2 < 64_500_000 and 3 * n <= 128 and planes == 4

time: 227 us -> 227 us (level)
  no operation moved by 1% of the time
where the time goes in v6:
time: 227 us
  Pallas kernels  222 us (98%)
  other arithmetic  3.35 us (1%)
    pallas_call x1, Pallas kernels, fused(): pl.pallas_call(functools.partial(fused_kernel, dims + (lax.axis_size('pip...  222 us

profile of v6, /device:TPU:0, one launch (start us, length us, event | category | flops | bytes accessed | tf_op | source)
XLA Modules:
  0.0 226.6 jit_solution(5527566973248795806)
XLA Ops:
  0.6 221.9 %shard_map.103 = (bf16[64,3584]{1,0:T(8,128)(2,1)}, bf16[64,3584]{1,0:T(8,128)(2,1)}, f32[2,3584]{1,0:T(2,128)}) custom-call(bf16[64,3584]{1,0:T(8,128)(2,1)} %bitcast.20, bf16[64,3584]{1,0:T(8,128)(2,1)} %bitcast.22, bf16[64,3584]{1,0:T(8,128)(2,1)} %bitcast.21, s32[8,64]{1,0:T(8,128)} %bitcast.24, s32[8,64]{1,0:T(8,128)} %bitcast.25, ...), custom_call_target="tpu_custom_call" | custom-call | tf_op jit(solution)/shard_map/pallas_call | solution.py:1263
  222.6 2.6 %fusion = (bf16[1,64,3584]{2,1,0:T(8,128)(2,1)}, bf16[1,64,3584]{2,1,0:T(8,128)(2,1)}) fusion(bf16[64,3584]{1,0:T(8,128)(2,1)} %get-tuple-element.6, bf16[1,64,3584]{2,1,0:T(8,128)(2,1)} %param.8, bf16[64,3584]{1,0:T(8,128)(2,1)} %get-tuple-element.7, bf16[1,64,3584]{2,1,0:T(8,128)(2,1)} %param.12), kind=kLoop, calls=%fused_computation.2 | loop fusion | flops 1835008 | bytes 2752512 | tf_op jit(solution)/shard_map/broadcast_in_dim | solution.py:1296
  225.2 0.8 reduce_sum.9
  225.9 0.6 broadcast_in_dim.11
